TPU v7x, 512 devices: a whole 4x4x16 slice. The times are simulated.
512 devices in a mesh: tm: 8 (over z_lo), gx: 16 (over y, x), gy: 4 (over z_hi, core).
Axes of the slice: x: 4, y: 4, z: 16 (z_hi: 2, z_lo: 8; z = z_hi * 8 + z_lo), core: 2. Of those that a mesh axis runs over, the one named last changes fastest.
Arguments:
- start_states: float32 [8, 512, 64, 256], P('tm', 'gx', 'gy'), may hold values from 0.5 to 2
- wind_code: int32 [16, 4], P('gx', 'gy'), may hold values from 0 to 7
- wind_profile: float32 [2, 256], replicated, may hold values from 0.05 to 0.4
- vertical_mix: float32 [512, 64, 256], P('gx', 'gy'), may hold values from 0.01 to 0.1
Outputs:
- middle_states: float32 [8, 512, 64, 256], P('tm', 'gx', 'gy')
- final_states: float32 [8, 512, 64, 256], P('tm', 'gx', 'gy')
Inputs may be any that keep to these rules, and one draw needn't show every extreme that they name: `wind_code`: a regime code.
All inputs are finite; a program needn't handle non-finite values.
Results may differ from a plain program's by a relative error of at most 0.00002.
Values sent between devices are 32-bit elements; how exact they have to be, the bound alone decides.
A program may use at most 64 MiB of HBM per device.

v0:
```python
import jax
import jax.numpy as jnp
from jax import lax
from jax.sharding import PartitionSpec as P

SWEEPS = 3


time_step = 0.5
half_step = 0.25
diffusion_low = 0.04
diffusion_high = 0.1
first_weights = (5.0 / 24.0, 1.0 / 3.0, -1.0 / 24.0)
second_weights = (-1.0 / 24.0, 1.0 / 3.0, 5.0 / 24.0)


def padded_2(x, sides, width):
    for axis, dim in sides:
        devices, length = (lax.axis_size(axis), x.shape[dim])
        up = [(i, (i + 1) % devices) for i in range(devices - 1)]
        down = [(j, i) for i, j in up]
        last = lax.slice_in_dim(x, length - width, length, axis=dim)
        initial = lax.slice_in_dim(x, 0, width, axis=dim)
        before = lax.ppermute(last, axis, up)
        after = lax.ppermute(initial, axis, down)
        x = jnp.concatenate([before, x, after], axis=dim)
    return x


def shifted(x, axis, by):
    devices = lax.axis_size(axis)
    pairs = [(i, i + by) for i in range(devices) if 0 <= i + by < devices]
    return lax.ppermute(x, axis, pairs)


def tendency(padded, sign_x, sign_y, strength, wind_profile, vertical_mix):
    row_count = padded.shape[0] - 4
    columns = padded.shape[1] - 4

    def neighbour(source, step_x, step_y):
        return source[2 + step_x : 2 + step_x + row_count, 2 + step_y : 2 + step_y + columns]

    centre = neighbour(padded, 0, 0)
    squared = padded * padded
    growth = squared / (1.0 + squared)
    growth_centre = neighbour(growth, 0, 0)
    spread = jnp.zeros_like(centre)
    for step_x, step_y in ((1, 0), (-1, 0), (0, 1), (0, -1)):
        weight = 0.5 + 0.5 * (growth_centre + neighbour(growth, step_x, step_y))
        spread = spread + weight * (neighbour(padded, step_x, step_y) - centre)
    upwind_x = jnp.where(sign_x > 0, neighbour(padded, -1, 0), neighbour(padded, 1, 0))
    farther_x = jnp.where(sign_x > 0, neighbour(padded, -2, 0), neighbour(padded, 2, 0))
    upwind_y = jnp.where(sign_y > 0, neighbour(padded, 0, -1), neighbour(padded, 0, 1))
    farther_y = jnp.where(sign_y > 0, neighbour(padded, 0, -2), neighbour(padded, 0, 2))
    carried = wind_profile[0] * (3.0 * centre - 4.0 * upwind_x + farther_x)
    carried = carried + wind_profile[1] * (3.0 * centre - 4.0 * upwind_y + farther_y)
    below_cells = jnp.concatenate([centre[:, :, :1], centre[:, :, :-1]], axis=2)
    above_cells = jnp.concatenate([centre[:, :, 1:], centre[:, :, -1:]], axis=2)
    return (
        strength * spread
        - 0.5 * carried
        + vertical_mix * (below_cells + above_cells - 2.0 * centre)
    )


def sweep_once(first_state, first_rate, slopes, tendency_of):
    middle = (
        first_state
        + half_step * (first_rate - slopes[0])
        + time_step
        * (
            first_weights[0] * slopes[0]
            + first_weights[1] * slopes[1]
            + first_weights[2] * slopes[2]
        )
    )
    middle_rate = tendency_of(middle)
    final_state = (
        middle
        + half_step * (middle_rate - slopes[1])
        + time_step
        * (
            second_weights[0] * slopes[0]
            + second_weights[1] * slopes[1]
            + second_weights[2] * slopes[2]
        )
    )
    final_rate = tendency_of(final_state)
    return ((first_state, middle, final_state), (first_rate, middle_rate, final_rate))


def shards(start_states, wind_code, wind_profile, vertical_mix):
    initial_state = start_states[0]
    regime = wind_code[0, 0]
    sign_x = 1.0 - 2.0 * (regime % 2).astype(jnp.float32)
    sign_y = 1.0 - 2.0 * (regime // 2 % 2).astype(jnp.float32)
    strength = jnp.where(regime // 4 == 1, diffusion_high, diffusion_low)

    def tendency_of(state_field):
        padded = padded_2(state_field, (("gx", 0), ("gy", 1)), 2)
        return tendency(padded, sign_x, sign_y, strength, wind_profile, vertical_mix)

    first_slice = lax.axis_index("tm") == 0
    initial_rate = tendency_of(initial_state)
    states = (initial_state, initial_state, initial_state)
    slopes = (initial_rate, initial_rate, initial_rate)
    for sweep_index in range(SWEEPS):
        arrived = shifted(states[2], "tm", 1)
        first_state = jnp.where(first_slice, initial_state, arrived)
        first_rate = initial_rate
        first_state, first_rate = (first_state, first_rate)
        first_rate = tendency_of(first_state)
        states, slopes = sweep_once(first_state, first_rate, slopes, tendency_of)
    return (states[1][None], states[2][None])


def solution(mesh):
    in_specs = (P("tm", "gx", "gy", None), P("gx", "gy"), P(), P("gx", "gy", None))
    out_specs = (P("tm", "gx", "gy", None), P("tm", "gx", "gy", None))
    return jax.shard_map(shards, mesh=mesh, in_specs=in_specs, out_specs=out_specs, check_vma=False)
```

profile of v0, /device:TPU:7, one launch (start us, length us, event | category | flops | bytes accessed | tf_op | source)
XLA Modules:
  0.0 286.2 jit_solution(4965297110315588840)
XLA Ops:
  6.7 3.7 %collective-permute-start = (f32[32,16,256]{2,1,0:T(8,128)}, f32[32,16,256]{2,1,0:T(8,128)S(1)}, u32[]{:S(2)}, u32[]{:S(2)}) collective-permute-start(f32[32,16,256]{2,1,0:T(8,128)} %bitcast.18), channel_id=1, source_target_pairs={{0,64},{64,128},{128,192},{192,256},{256,320},{320,384},{384,448},... | collective-permute-start | bytes 1572872 | tf_op jit(solution)/shard_map/ppermute | solution.py:33
  12.2 16.6 %collective-permute-start.7 = (f32[36,2,256]{2,1,0:T(2,128)S(1)}, f32[36,2,256]{2,1,0:T(2,128)S(1)}, u32[]{:S(2)}, u32[]{:S(2)}) collective-permute-start(f32[36,2,256]{2,1,0:T(2,128)S(1)} %get-tuple-element.44), channel_id=1, source_target_pairs={{0,1},{1,2},{2,3},{4,5},{5,6},{6,7},{8,9},{9,10},{10,11},{12,13},{... | collective-permute-start | bytes 221192 | tf_op jit(solution)/shard_map/ppermute | solution.py:24
  31.5 11.7 %collective-permute-done.8 = f32[36,2,256]{2,1,0:T(2,128)S(1)} collective-permute-done((f32[36,2,256]{2,1,0:T(2,128)S(1)}, f32[36,2,256]{2,1,0:T(2,128)S(1)}, u32[]{:S(2)}, u32[]{:S(2)}) %collective-permute-start.8) | collective-permute-done | bytes 73760 | tf_op jit(solution)/shard_map/ppermute | solution.py:25
  43.7 4.6 %collective-permute-start.1 = (f32[2,16,256]{2,1,0:T(8,128)S(1)}, f32[2,16,256]{2,1,0:T(8,128)S(1)}, u32[]{:S(2)}, u32[]{:S(2)}) collective-permute-start(f32[2,16,256]{2,1,0:T(8,128)S(1)} %get-tuple-element.98), channel_id=1, source_target_pairs={{0,4},{4,8},{8,12},{12,16},{16,20},{20,24},{24,28},{28,32},{32,36}... | collective-permute-start | bytes 98312 | tf_op jit(solution)/shard_map/ppermute | solution.py:24
  50.4 4.6 %collective-permute-done.2 = f32[2,16,256]{2,1,0:T(8,128)S(1)} collective-permute-done((f32[2,16,256]{2,1,0:T(8,128)S(1)}, f32[2,16,256]{2,1,0:T(8,128)S(1)}, u32[]{:S(2)}, u32[]{:S(2)}) %collective-permute-start.2) | collective-permute-done | bytes 32800 | tf_op jit(solution)/shard_map/ppermute | solution.py:25
  55.1 3.3 %collective-permute-start.3 = (f32[36,2,256]{2,1,0:T(2,128)S(1)}, f32[36,2,256]{2,1,0:T(2,128)S(1)}, u32[]{:S(2)}, u32[]{:S(2)}) collective-permute-start(f32[36,2,256]{2,1,0:T(2,128)S(1)} %get-tuple-element.48), channel_id=1, source_target_pairs={{0,1},{1,2},{2,3},{4,5},{5,6},{6,7},{8,9},{9,10},{10,11},{12,13},{... | collective-permute-start | bytes 221192 | tf_op jit(solution)/shard_map/ppermute | solution.py:24
  60.5 12.3 %collective-permute-done.4 = f32[36,2,256]{2,1,0:T(2,128)S(1)} collective-permute-done((f32[36,2,256]{2,1,0:T(2,128)S(1)}, f32[36,2,256]{2,1,0:T(2,128)S(1)}, u32[]{:S(2)}, u32[]{:S(2)}) %collective-permute-start.4) | collective-permute-done | bytes 73760 | tf_op jit(solution)/shard_map/ppermute | solution.py:25
  74.1 3.2 %multiply_add_fusion.3 = (f32[32,16,256]{2,1,0:T(8,128)S(1)}, f32[32,16,256]{2,1,0:T(8,128)S(1)}, f32[32,16,256]{2,1,0:T(8,128)S(1)}) fusion(f32[32,16,256]{2,1,0:T(8,128)S(1)} %broadcast_select_fusion.2, f32[32,16,256]{2,1,0:T(8,128)S(1)} %copy-done.2, f32[32,16,1]{2,1,0:T(8,128)S(1)} %get-tuple-element.101, f32[32,16,255]{2,1,0:T(8,128)S(1)} %get-tuple-element.103, ...), kind=kLoop, calls=%fused_computation.417 | loop fusion | flops 14680064 | bytes 14813190 | tf_op jit(solution)/shard_map/add | solution.py:68
  79.2 3.4 %collective-permute-start.10 = (f32[2,16,256]{2,1,0:T(8,128)S(1)}, f32[2,16,256]{2,1,0:T(8,128)S(1)}, u32[]{:S(2)}, u32[]{:S(2)}) collective-permute-start(f32[2,16,256]{2,1,0:T(8,128)S(1)} %get-tuple-element.87), channel_id=1, source_target_pairs={{4,0},{8,4},{12,8},{16,12},{20,16},{24,20},{28,24},{32,28},{36,32}... | collective-permute-start | bytes 98312 | tf_op jit(solution)/shard_map/ppermute | solution.py:25
  82.8 3.2 %collective-permute-done.10 = f32[2,16,256]{2,1,0:T(8,128)S(1)} collective-permute-done((f32[2,16,256]{2,1,0:T(8,128)S(1)}, f32[2,16,256]{2,1,0:T(8,128)S(1)}, u32[]{:S(2)}, u32[]{:S(2)}) %collective-permute-start.10) | collective-permute-done | bytes 32800 | tf_op jit(solution)/shard_map/ppermute | solution.py:25
  91.1 13.1 %collective-permute-done.12 = f32[36,2,256]{2,1,0:T(2,128)S(1)} collective-permute-done((f32[36,2,256]{2,1,0:T(2,128)S(1)}, f32[36,2,256]{2,1,0:T(2,128)S(1)}, u32[]{:S(2)}, u32[]{:S(2)}) %collective-permute-start.12) | collective-permute-done | bytes 73760 | tf_op jit(solution)/shard_map/ppermute | solution.py:25
  110.3 3.4 %collective-permute-start.19 = (f32[2,16,256]{2,1,0:T(8,128)S(1)}, f32[2,16,256]{2,1,0:T(8,128)S(1)}, u32[]{:S(2)}, u32[]{:S(2)}) collective-permute-start(f32[2,16,256]{2,1,0:T(8,128)S(1)} %get-tuple-element.75), channel_id=1, source_target_pairs={{4,0},{8,4},{12,8},{16,12},{20,16},{24,20},{28,24},{32,28},{36,32}... | collective-permute-start | bytes 98312 | tf_op jit(solution)/shard_map/ppermute | solution.py:25
  113.9 3.2 %collective-permute-done.19 = f32[2,16,256]{2,1,0:T(8,128)S(1)} collective-permute-done((f32[2,16,256]{2,1,0:T(8,128)S(1)}, f32[2,16,256]{2,1,0:T(8,128)S(1)}, u32[]{:S(2)}, u32[]{:S(2)}) %collective-permute-start.19) | collective-permute-done | bytes 32800 | tf_op jit(solution)/shard_map/ppermute | solution.py:25
  117.2 3.3 %collective-permute-start.20 = (f32[36,2,256]{2,1,0:T(2,128)S(1)}, f32[36,2,256]{2,1,0:T(2,128)S(1)}, u32[]{:S(2)}, u32[]{:S(2)}) collective-permute-start(f32[36,2,256]{2,1,0:T(2,128)S(1)} %get-tuple-element.32), channel_id=1, source_target_pairs={{0,1},{1,2},{2,3},{4,5},{5,6},{6,7},{8,9},{9,10},{10,11},{12,13},{... | collective-permute-start | bytes 221192 | tf_op jit(solution)/shard_map/ppermute | solution.py:24
  122.5 12.3 %collective-permute-done.21 = f32[36,2,256]{2,1,0:T(2,128)S(1)} collective-permute-done((f32[36,2,256]{2,1,0:T(2,128)S(1)}, f32[36,2,256]{2,1,0:T(2,128)S(1)}, u32[]{:S(2)}, u32[]{:S(2)}) %collective-permute-start.21) | collective-permute-done | bytes 73760 | tf_op jit(solution)/shard_map/ppermute | solution.py:25
  137.3 3.4 %collective-permute-start.15 = (f32[2,16,256]{2,1,0:T(8,128)S(1)}, f32[2,16,256]{2,1,0:T(8,128)S(1)}, u32[]{:S(2)}, u32[]{:S(2)}) collective-permute-start(f32[2,16,256]{2,1,0:T(8,128)S(1)} %get-tuple-element.81), channel_id=1, source_target_pairs={{4,0},{8,4},{12,8},{16,12},{20,16},{24,20},{28,24},{32,28},{36,32}... | collective-permute-start | bytes 98312 | tf_op jit(solution)/shard_map/ppermute | solution.py:25
  140.9 3.2 %collective-permute-done.15 = f32[2,16,256]{2,1,0:T(8,128)S(1)} collective-permute-done((f32[2,16,256]{2,1,0:T(8,128)S(1)}, f32[2,16,256]{2,1,0:T(8,128)S(1)}, u32[]{:S(2)}, u32[]{:S(2)}) %collective-permute-start.15) | collective-permute-done | bytes 32800 | tf_op jit(solution)/shard_map/ppermute | solution.py:25
  149.2 12.3 %collective-permute-done.17 = f32[36,2,256]{2,1,0:T(2,128)S(1)} collective-permute-done((f32[36,2,256]{2,1,0:T(2,128)S(1)}, f32[36,2,256]{2,1,0:T(2,128)S(1)}, u32[]{:S(2)}, u32[]{:S(2)}) %collective-permute-start.17) | collective-permute-done | bytes 73760 | tf_op jit(solution)/shard_map/ppermute | solution.py:25
  161.9 3.4 %multiply_add_fusion.1 = (f32[32,16,256]{2,1,0:T(8,128)S(1)}, f32[32,16,256]{2,1,0:T(8,128)S(1)}, f32[32,16,256]{2,1,0:T(8,128)S(1)}) fusion(f32[32,16,256]{2,1,0:T(8,128)S(1)} %get-tuple-element.12, f32[32,16,256]{2,1,0:T(8,128)S(1)} %broadcast_select_fusion.1, f32[32,16,256]{2,1,0:T(8,128)S(1)} %get-tuple-element.10, f32[32,16,256]{2,1,0:T(8,128)S(1)} %copy-done.2, ...), kind=kLoop, calls=%fused_computation.415 | loop fusion | flops 14680064 | bytes 15861766 | tf_op jit(solution)/shard_map/add | solution.py:68
  167.3 3.4 %collective-permute-start.23 = (f32[2,16,256]{2,1,0:T(8,128)S(1)}, f32[2,16,256]{2,1,0:T(8,128)S(1)}, u32[]{:S(2)}, u32[]{:S(2)}) collective-permute-start(f32[2,16,256]{2,1,0:T(8,128)S(1)} %get-tuple-element.69), channel_id=1, source_target_pairs={{4,0},{8,4},{12,8},{16,12},{20,16},{24,20},{28,24},{32,28},{36,32}... | collective-permute-start | bytes 98312 | tf_op jit(solution)/shard_map/ppermute | solution.py:25
  170.8 3.2 %collective-permute-done.23 = f32[2,16,256]{2,1,0:T(8,128)S(1)} collective-permute-done((f32[2,16,256]{2,1,0:T(8,128)S(1)}, f32[2,16,256]{2,1,0:T(8,128)S(1)}, u32[]{:S(2)}, u32[]{:S(2)}) %collective-permute-start.23) | collective-permute-done | bytes 32800 | tf_op jit(solution)/shard_map/ppermute | solution.py:25
  179.2 13.1 %collective-permute-done.25 = f32[36,2,256]{2,1,0:T(2,128)S(1)} collective-permute-done((f32[36,2,256]{2,1,0:T(2,128)S(1)}, f32[36,2,256]{2,1,0:T(2,128)S(1)}, u32[]{:S(2)}, u32[]{:S(2)}) %collective-permute-start.25) | collective-permute-done | bytes 73760 | tf_op jit(solution)/shard_map/ppermute | solution.py:25
  194.5 5.9 %collective-permute-start.26 = (f32[32,16,256]{2,1,0:T(8,128)S(1)}, f32[32,16,256]{2,1,0:T(8,128)S(1)}, u32[]{:S(2)}, u32[]{:S(2)}) collective-permute-start(f32[32,16,256]{2,1,0:T(8,128)S(1)} %get-tuple-element.4), channel_id=1, source_target_pairs={{0,64},{64,128},{128,192},{192,256},{256,320},{320,384},{384,448},... | collective-permute-start | bytes 1572872 | tf_op jit(solution)/shard_map/ppermute | solution.py:33
  202.3 3.5 %collective-permute-start.32 = (f32[2,16,256]{2,1,0:T(8,128)S(1)}, f32[2,16,256]{2,1,0:T(8,128)S(1)}, u32[]{:S(2)}, u32[]{:S(2)}) collective-permute-start(f32[2,16,256]{2,1,0:T(8,128)S(1)} %get-tuple-element.57), channel_id=1, source_target_pairs={{4,0},{8,4},{12,8},{16,12},{20,16},{24,20},{28,24},{32,28},{36,32}... | collective-permute-start | bytes 98312 | tf_op jit(solution)/shard_map/ppermute | solution.py:25
  214.4 12.3 %collective-permute-done.34 = f32[36,2,256]{2,1,0:T(2,128)S(1)} collective-permute-done((f32[36,2,256]{2,1,0:T(2,128)S(1)}, f32[36,2,256]{2,1,0:T(2,128)S(1)}, u32[]{:S(2)}, u32[]{:S(2)}) %collective-permute-start.34) | collective-permute-done | bytes 73760 | tf_op jit(solution)/shard_map/ppermute | solution.py:25
  229.2 3.4 %collective-permute-start.28 = (f32[2,16,256]{2,1,0:T(8,128)S(1)}, f32[2,16,256]{2,1,0:T(8,128)S(1)}, u32[]{:S(2)}, u32[]{:S(2)}) collective-permute-start(f32[2,16,256]{2,1,0:T(8,128)S(1)} %get-tuple-element.67), channel_id=1, source_target_pairs={{4,0},{8,4},{12,8},{16,12},{20,16},{24,20},{28,24},{32,28},{36,32}... | collective-permute-start | bytes 98312 | tf_op jit(solution)/shard_map/ppermute | solution.py:25
  232.7 3.2 %collective-permute-done.28 = f32[2,16,256]{2,1,0:T(8,128)S(1)} collective-permute-done((f32[2,16,256]{2,1,0:T(8,128)S(1)}, f32[2,16,256]{2,1,0:T(8,128)S(1)}, u32[]{:S(2)}, u32[]{:S(2)}) %collective-permute-start.28) | collective-permute-done | bytes 32800 | tf_op jit(solution)/shard_map/ppermute | solution.py:25
  241.1 12.3 %collective-permute-done.30 = f32[36,2,256]{2,1,0:T(2,128)S(1)} collective-permute-done((f32[36,2,256]{2,1,0:T(2,128)S(1)}, f32[36,2,256]{2,1,0:T(2,128)S(1)}, u32[]{:S(2)}, u32[]{:S(2)}) %collective-permute-start.30) | collective-permute-done | bytes 73760 | tf_op jit(solution)/shard_map/ppermute | solution.py:25
  253.8 3.3 %fusion.82 = (f32[32,16,256]{2,1,0:T(8,128)S(1)}, f32[32,16,256]{2,1,0:T(8,128)S(1)}) fusion(f32[32,16,256]{2,1,0:T(8,128)S(1)} %broadcast_select_fusion, f32[32,16,256]{2,1,0:T(8,128)S(1)} %get-tuple-element.7, f32[36,18,256]{2,1,0:T(8,128)S(1)} %get-tuple-element.23, f32[36,18,256]{2,1,0:T(8,128)S(1)} %get-tuple-element.22, ...), kind=kLoop, calls=%fused_computation.169 | loop fusion | flops 14680064 | bytes 15337478 | tf_op jit(solution)/shard_map/add | solution.py:68
  259.1 3.4 %collective-permute-start.36 = (f32[2,16,256]{2,1,0:T(8,128)S(1)}, f32[2,16,256]{2,1,0:T(8,128)S(1)}, u32[]{:S(2)}, u32[]{:S(2)}) collective-permute-start(f32[2,16,256]{2,1,0:T(8,128)S(1)} %get-tuple-element.55), channel_id=1, source_target_pairs={{4,0},{8,4},{12,8},{16,12},{20,16},{24,20},{28,24},{32,28},{36,32}... | collective-permute-start | bytes 98312 | tf_op jit(solution)/shard_map/ppermute | solution.py:25
  262.6 3.2 %collective-permute-done.36 = f32[2,16,256]{2,1,0:T(8,128)S(1)} collective-permute-done((f32[2,16,256]{2,1,0:T(8,128)S(1)}, f32[2,16,256]{2,1,0:T(8,128)S(1)}, u32[]{:S(2)}, u32[]{:S(2)}) %collective-permute-start.36) | collective-permute-done | bytes 32800 | tf_op jit(solution)/shard_map/ppermute | solution.py:25
  271.0 12.3 %collective-permute-done.38 = f32[36,2,256]{2,1,0:T(2,128)S(1)} collective-permute-done((f32[36,2,256]{2,1,0:T(2,128)S(1)}, f32[36,2,256]{2,1,0:T(2,128)S(1)}, u32[]{:S(2)}, u32[]{:S(2)}) %collective-permute-start.38) | collective-permute-done | bytes 73760 | tf_op jit(solution)/shard_map/ppermute | solution.py:25
  (118 shorter events, 77.5 us)
Async XLA Ops:
  1.4 10.7 %collective-permute-start.5 = (f32[2,16,256]{2,1,0:T(8,128)S(1)}, f32[2,16,256]{2,1,0:T(8,128)S(1)}, u32[]{:S(2)}, u32[]{:S(2)}) collective-permute-start(f32[2,16,256]{2,1,0:T(8,128)S(1)} %get-tuple-element.92), channel_id=1, source_target_pairs={{0,4},{4,8},{8,12},{12,16},{16,20},{20,24},{24,28},{28,32},{32,36}... | collective-permute-start | bytes 98312 | tf_op jit(solution)/shard_map/ppermute | solution.py:24
  4.5 7.6 %collective-permute-start.6 = (f32[2,16,256]{2,1,0:T(8,128)S(1)}, f32[2,16,256]{2,1,0:T(8,128)S(1)}, u32[]{:S(2)}, u32[]{:S(2)}) collective-permute-start(f32[2,16,256]{2,1,0:T(8,128)S(1)} %get-tuple-element.93), channel_id=1, source_target_pairs={{4,0},{8,4},{12,8},{16,12},{20,16},{24,20},{28,24},{32,28},{36,32}... | collective-permute-start | bytes 98312 | tf_op jit(solution)/shard_map/ppermute | solution.py:25
  6.7 36.9 %collective-permute-start = (f32[32,16,256]{2,1,0:T(8,128)}, f32[32,16,256]{2,1,0:T(8,128)S(1)}, u32[]{:S(2)}, u32[]{:S(2)}) collective-permute-start(f32[32,16,256]{2,1,0:T(8,128)} %bitcast.18), channel_id=1, source_target_pairs={{0,64},{64,128},{128,192},{192,256},{256,320},{320,384},{384,448},... | collective-permute-start | bytes 1572872 | tf_op jit(solution)/shard_map/ppermute | solution.py:33
  12.2 19.3 %collective-permute-start.7 = (f32[36,2,256]{2,1,0:T(2,128)S(1)}, f32[36,2,256]{2,1,0:T(2,128)S(1)}, u32[]{:S(2)}, u32[]{:S(2)}) collective-permute-start(f32[36,2,256]{2,1,0:T(2,128)S(1)} %get-tuple-element.44), channel_id=1, source_target_pairs={{0,1},{1,2},{2,3},{4,5},{5,6},{6,7},{8,9},{9,10},{10,11},{12,13},{... | collective-permute-start | bytes 221192 | tf_op jit(solution)/shard_map/ppermute | solution.py:24
  28.8 14.4 %collective-permute-start.8 = (f32[36,2,256]{2,1,0:T(2,128)S(1)}, f32[36,2,256]{2,1,0:T(2,128)S(1)}, u32[]{:S(2)}, u32[]{:S(2)}) collective-permute-start(f32[36,2,256]{2,1,0:T(2,128)S(1)} %get-tuple-element.45), channel_id=1, source_target_pairs={{1,0},{2,1},{3,2},{5,4},{6,5},{7,6},{9,8},{10,9},{11,10},{13,12},{... | collective-permute-start | bytes 221192 | tf_op jit(solution)/shard_map/ppermute | solution.py:25
  43.7 6.7 %collective-permute-start.1 = (f32[2,16,256]{2,1,0:T(8,128)S(1)}, f32[2,16,256]{2,1,0:T(8,128)S(1)}, u32[]{:S(2)}, u32[]{:S(2)}) collective-permute-start(f32[2,16,256]{2,1,0:T(8,128)S(1)} %get-tuple-element.98), channel_id=1, source_target_pairs={{0,4},{4,8},{8,12},{12,16},{16,20},{20,24},{24,28},{28,32},{32,36}... | collective-permute-start | bytes 98312 | tf_op jit(solution)/shard_map/ppermute | solution.py:24
  48.3 6.8 %collective-permute-start.2 = (f32[2,16,256]{2,1,0:T(8,128)S(1)}, f32[2,16,256]{2,1,0:T(8,128)S(1)}, u32[]{:S(2)}, u32[]{:S(2)}) collective-permute-start(f32[2,16,256]{2,1,0:T(8,128)S(1)} %get-tuple-element.99), channel_id=1, source_target_pairs={{4,0},{8,4},{12,8},{16,12},{20,16},{24,20},{28,24},{32,28},{36,32}... | collective-permute-start | bytes 98312 | tf_op jit(solution)/shard_map/ppermute | solution.py:25
  55.1 5.4 %collective-permute-start.3 = (f32[36,2,256]{2,1,0:T(2,128)S(1)}, f32[36,2,256]{2,1,0:T(2,128)S(1)}, u32[]{:S(2)}, u32[]{:S(2)}) collective-permute-start(f32[36,2,256]{2,1,0:T(2,128)S(1)} %get-tuple-element.48), channel_id=1, source_target_pairs={{0,1},{1,2},{2,3},{4,5},{5,6},{6,7},{8,9},{9,10},{10,11},{12,13},{... | collective-permute-start | bytes 221192 | tf_op jit(solution)/shard_map/ppermute | solution.py:24
  58.4 14.4 %collective-permute-start.4 = (f32[36,2,256]{2,1,0:T(2,128)S(1)}, f32[36,2,256]{2,1,0:T(2,128)S(1)}, u32[]{:S(2)}, u32[]{:S(2)}) collective-permute-start(f32[36,2,256]{2,1,0:T(2,128)S(1)} %get-tuple-element.49), channel_id=1, source_target_pairs={{1,0},{2,1},{3,2},{5,4},{6,5},{7,6},{9,8},{10,9},{11,10},{13,12},{... | collective-permute-start | bytes 221192 | tf_op jit(solution)/shard_map/ppermute | solution.py:25
  77.3 5.5 %collective-permute-start.9 = (f32[2,16,256]{2,1,0:T(8,128)S(1)}, f32[2,16,256]{2,1,0:T(8,128)S(1)}, u32[]{:S(2)}, u32[]{:S(2)}) collective-permute-start(f32[2,16,256]{2,1,0:T(8,128)S(1)} %get-tuple-element.86), channel_id=1, source_target_pairs={{0,4},{4,8},{8,12},{12,16},{16,20},{20,24},{24,28},{28,32},{32,36}... | collective-permute-start | bytes 98312 | tf_op jit(solution)/shard_map/ppermute | solution.py:24
  79.2 6.8 %collective-permute-start.10 = (f32[2,16,256]{2,1,0:T(8,128)S(1)}, f32[2,16,256]{2,1,0:T(8,128)S(1)}, u32[]{:S(2)}, u32[]{:S(2)}) collective-permute-start(f32[2,16,256]{2,1,0:T(8,128)S(1)} %get-tuple-element.87), channel_id=1, source_target_pairs={{4,0},{8,4},{12,8},{16,12},{20,16},{24,20},{28,24},{32,28},{36,32}... | collective-permute-start | bytes 98312 | tf_op jit(solution)/shard_map/ppermute | solution.py:25
  89.1 15.2 %collective-permute-start.12 = (f32[36,2,256]{2,1,0:T(2,128)S(1)}, f32[36,2,256]{2,1,0:T(2,128)S(1)}, u32[]{:S(2)}, u32[]{:S(2)}) collective-permute-start(f32[36,2,256]{2,1,0:T(2,128)S(1)} %get-tuple-element.41), channel_id=1, source_target_pairs={{1,0},{2,1},{3,2},{5,4},{6,5},{7,6},{9,8},{10,9},{11,10},{13,12},{... | collective-permute-start | bytes 221192 | tf_op jit(solution)/shard_map/ppermute | solution.py:25
  106.5 28.7 %collective-permute-start.13 = (f32[32,16,256]{2,1,0:T(8,128)S(1)}, f32[32,16,256]{2,1,0:T(8,128)S(1)}, u32[]{:S(2)}, u32[]{:S(2)}) collective-permute-start(f32[32,16,256]{2,1,0:T(8,128)S(1)} %get-tuple-element.9), channel_id=1, source_target_pairs={{0,64},{64,128},{128,192},{192,256},{256,320},{320,384},{384,448},... | collective-permute-start | bytes 1572872 | tf_op jit(solution)/shard_map/ppermute | solution.py:33
  108.4 5.5 %collective-permute-start.18 = (f32[2,16,256]{2,1,0:T(8,128)S(1)}, f32[2,16,256]{2,1,0:T(8,128)S(1)}, u32[]{:S(2)}, u32[]{:S(2)}) collective-permute-start(f32[2,16,256]{2,1,0:T(8,128)S(1)} %get-tuple-element.74), channel_id=1, source_target_pairs={{0,4},{4,8},{8,12},{12,16},{16,20},{20,24},{24,28},{28,32},{32,36}... | collective-permute-start | bytes 98312 | tf_op jit(solution)/shard_map/ppermute | solution.py:24
  110.3 6.8 %collective-permute-start.19 = (f32[2,16,256]{2,1,0:T(8,128)S(1)}, f32[2,16,256]{2,1,0:T(8,128)S(1)}, u32[]{:S(2)}, u32[]{:S(2)}) collective-permute-start(f32[2,16,256]{2,1,0:T(8,128)S(1)} %get-tuple-element.75), channel_id=1, source_target_pairs={{4,0},{8,4},{12,8},{16,12},{20,16},{24,20},{28,24},{32,28},{36,32}... | collective-permute-start | bytes 98312 | tf_op jit(solution)/shard_map/ppermute | solution.py:25
  120.5 14.4 %collective-permute-start.21 = (f32[36,2,256]{2,1,0:T(2,128)S(1)}, f32[36,2,256]{2,1,0:T(2,128)S(1)}, u32[]{:S(2)}, u32[]{:S(2)}) collective-permute-start(f32[36,2,256]{2,1,0:T(2,128)S(1)} %get-tuple-element.33), channel_id=1, source_target_pairs={{1,0},{2,1},{3,2},{5,4},{6,5},{7,6},{9,8},{10,9},{11,10},{13,12},{... | collective-permute-start | bytes 221192 | tf_op jit(solution)/shard_map/ppermute | solution.py:25
  135.3 5.5 %collective-permute-start.14 = (f32[2,16,256]{2,1,0:T(8,128)S(1)}, f32[2,16,256]{2,1,0:T(8,128)S(1)}, u32[]{:S(2)}, u32[]{:S(2)}) collective-permute-start(f32[2,16,256]{2,1,0:T(8,128)S(1)} %get-tuple-element.80), channel_id=1, source_target_pairs={{0,4},{4,8},{8,12},{12,16},{16,20},{20,24},{24,28},{28,32},{32,36}... | collective-permute-start | bytes 98312 | tf_op jit(solution)/shard_map/ppermute | solution.py:24
  137.3 6.8 %collective-permute-start.15 = (f32[2,16,256]{2,1,0:T(8,128)S(1)}, f32[2,16,256]{2,1,0:T(8,128)S(1)}, u32[]{:S(2)}, u32[]{:S(2)}) collective-permute-start(f32[2,16,256]{2,1,0:T(8,128)S(1)} %get-tuple-element.81), channel_id=1, source_target_pairs={{4,0},{8,4},{12,8},{16,12},{20,16},{24,20},{28,24},{32,28},{36,32}... | collective-permute-start | bytes 98312 | tf_op jit(solution)/shard_map/ppermute | solution.py:25
  147.1 14.4 %collective-permute-start.17 = (f32[36,2,256]{2,1,0:T(2,128)S(1)}, f32[36,2,256]{2,1,0:T(2,128)S(1)}, u32[]{:S(2)}, u32[]{:S(2)}) collective-permute-start(f32[36,2,256]{2,1,0:T(2,128)S(1)} %get-tuple-element.37), channel_id=1, source_target_pairs={{1,0},{2,1},{3,2},{5,4},{6,5},{7,6},{9,8},{10,9},{11,10},{13,12},{... | collective-permute-start | bytes 221192 | tf_op jit(solution)/shard_map/ppermute | solution.py:25
  165.3 5.5 %collective-permute-start.22 = (f32[2,16,256]{2,1,0:T(8,128)S(1)}, f32[2,16,256]{2,1,0:T(8,128)S(1)}, u32[]{:S(2)}, u32[]{:S(2)}) collective-permute-start(f32[2,16,256]{2,1,0:T(8,128)S(1)} %get-tuple-element.68), channel_id=1, source_target_pairs={{0,4},{4,8},{8,12},{12,16},{16,20},{20,24},{24,28},{28,32},{32,36}... | collective-permute-start | bytes 98312 | tf_op jit(solution)/shard_map/ppermute | solution.py:24
  167.3 6.8 %collective-permute-start.23 = (f32[2,16,256]{2,1,0:T(8,128)S(1)}, f32[2,16,256]{2,1,0:T(8,128)S(1)}, u32[]{:S(2)}, u32[]{:S(2)}) collective-permute-start(f32[2,16,256]{2,1,0:T(8,128)S(1)} %get-tuple-element.69), channel_id=1, source_target_pairs={{4,0},{8,4},{12,8},{16,12},{20,16},{24,20},{28,24},{32,28},{36,32}... | collective-permute-start | bytes 98312 | tf_op jit(solution)/shard_map/ppermute | solution.py:25
  177.1 15.2 %collective-permute-start.25 = (f32[36,2,256]{2,1,0:T(2,128)S(1)}, f32[36,2,256]{2,1,0:T(2,128)S(1)}, u32[]{:S(2)}, u32[]{:S(2)}) collective-permute-start(f32[36,2,256]{2,1,0:T(2,128)S(1)} %get-tuple-element.29), channel_id=1, source_target_pairs={{1,0},{2,1},{3,2},{5,4},{6,5},{7,6},{9,8},{10,9},{11,10},{13,12},{... | collective-permute-start | bytes 221192 | tf_op jit(solution)/shard_map/ppermute | solution.py:25
  194.5 32.6 %collective-permute-start.26 = (f32[32,16,256]{2,1,0:T(8,128)S(1)}, f32[32,16,256]{2,1,0:T(8,128)S(1)}, u32[]{:S(2)}, u32[]{:S(2)}) collective-permute-start(f32[32,16,256]{2,1,0:T(8,128)S(1)} %get-tuple-element.4), channel_id=1, source_target_pairs={{0,64},{64,128},{128,192},{192,256},{256,320},{320,384},{384,448},... | collective-permute-start | bytes 1572872 | tf_op jit(solution)/shard_map/ppermute | solution.py:33
  200.4 5.7 %collective-permute-start.31 = (f32[2,16,256]{2,1,0:T(8,128)S(1)}, f32[2,16,256]{2,1,0:T(8,128)S(1)}, u32[]{:S(2)}, u32[]{:S(2)}) collective-permute-start(f32[2,16,256]{2,1,0:T(8,128)S(1)} %get-tuple-element.56), channel_id=1, source_target_pairs={{0,4},{4,8},{8,12},{12,16},{16,20},{20,24},{24,28},{28,32},{32,36}... | collective-permute-start | bytes 98312 | tf_op jit(solution)/shard_map/ppermute | solution.py:24
  202.3 6.8 %collective-permute-start.32 = (f32[2,16,256]{2,1,0:T(8,128)S(1)}, f32[2,16,256]{2,1,0:T(8,128)S(1)}, u32[]{:S(2)}, u32[]{:S(2)}) collective-permute-start(f32[2,16,256]{2,1,0:T(8,128)S(1)} %get-tuple-element.57), channel_id=1, source_target_pairs={{4,0},{8,4},{12,8},{16,12},{20,16},{24,20},{28,24},{32,28},{36,32}... | collective-permute-start | bytes 98312 | tf_op jit(solution)/shard_map/ppermute | solution.py:25
  212.3 14.4 %collective-permute-start.34 = (f32[36,2,256]{2,1,0:T(2,128)S(1)}, f32[36,2,256]{2,1,0:T(2,128)S(1)}, u32[]{:S(2)}, u32[]{:S(2)}) collective-permute-start(f32[36,2,256]{2,1,0:T(2,128)S(1)} %get-tuple-element.21), channel_id=1, source_target_pairs={{1,0},{2,1},{3,2},{5,4},{6,5},{7,6},{9,8},{10,9},{11,10},{13,12},{... | collective-permute-start | bytes 221192 | tf_op jit(solution)/shard_map/ppermute | solution.py:25
  227.2 5.5 %collective-permute-start.27 = (f32[2,16,256]{2,1,0:T(8,128)S(1)}, f32[2,16,256]{2,1,0:T(8,128)S(1)}, u32[]{:S(2)}, u32[]{:S(2)}) collective-permute-start(f32[2,16,256]{2,1,0:T(8,128)S(1)} %get-tuple-element.66), channel_id=1, source_target_pairs={{0,4},{4,8},{8,12},{12,16},{16,20},{20,24},{24,28},{28,32},{32,36}... | collective-permute-start | bytes 98312 | tf_op jit(solution)/shard_map/ppermute | solution.py:24
  229.2 6.8 %collective-permute-start.28 = (f32[2,16,256]{2,1,0:T(8,128)S(1)}, f32[2,16,256]{2,1,0:T(8,128)S(1)}, u32[]{:S(2)}, u32[]{:S(2)}) collective-permute-start(f32[2,16,256]{2,1,0:T(8,128)S(1)} %get-tuple-element.67), channel_id=1, source_target_pairs={{4,0},{8,4},{12,8},{16,12},{20,16},{24,20},{28,24},{32,28},{36,32}... | collective-permute-start | bytes 98312 | tf_op jit(solution)/shard_map/ppermute | solution.py:25
  239.0 14.4 %collective-permute-start.30 = (f32[36,2,256]{2,1,0:T(2,128)S(1)}, f32[36,2,256]{2,1,0:T(2,128)S(1)}, u32[]{:S(2)}, u32[]{:S(2)}) collective-permute-start(f32[36,2,256]{2,1,0:T(2,128)S(1)} %get-tuple-element.25), channel_id=1, source_target_pairs={{1,0},{2,1},{3,2},{5,4},{6,5},{7,6},{9,8},{10,9},{11,10},{13,12},{... | collective-permute-start | bytes 221192 | tf_op jit(solution)/shard_map/ppermute | solution.py:25
  257.1 5.5 %collective-permute-start.35 = (f32[2,16,256]{2,1,0:T(8,128)S(1)}, f32[2,16,256]{2,1,0:T(8,128)S(1)}, u32[]{:S(2)}, u32[]{:S(2)}) collective-permute-start(f32[2,16,256]{2,1,0:T(8,128)S(1)} %get-tuple-element.54), channel_id=1, source_target_pairs={{0,4},{4,8},{8,12},{12,16},{16,20},{20,24},{24,28},{28,32},{32,36}... | collective-permute-start | bytes 98312 | tf_op jit(solution)/shard_map/ppermute | solution.py:24
  259.1 6.8 %collective-permute-start.36 = (f32[2,16,256]{2,1,0:T(8,128)S(1)}, f32[2,16,256]{2,1,0:T(8,128)S(1)}, u32[]{:S(2)}, u32[]{:S(2)}) collective-permute-start(f32[2,16,256]{2,1,0:T(8,128)S(1)} %get-tuple-element.55), channel_id=1, source_target_pairs={{4,0},{8,4},{12,8},{16,12},{20,16},{24,20},{28,24},{32,28},{36,32}... | collective-permute-start | bytes 98312 | tf_op jit(solution)/shard_map/ppermute | solution.py:25
  268.9 14.4 %collective-permute-start.38 = (f32[36,2,256]{2,1,0:T(2,128)S(1)}, f32[36,2,256]{2,1,0:T(2,128)S(1)}, u32[]{:S(2)}, u32[]{:S(2)}) collective-permute-start(f32[36,2,256]{2,1,0:T(2,128)S(1)} %get-tuple-element.17), channel_id=1, source_target_pairs={{1,0},{2,1},{3,2},{5,4},{6,5},{7,6},{9,8},{10,9},{11,10},{13,12},{... | collective-permute-start | bytes 221192 | tf_op jit(solution)/shard_map/ppermute | solution.py:25
  (11 other events, 87.4 us)
where the time goes:
time: 288 us; the launch traced here: 286 us
  waiting for transfers between devices  139 us (48%)
  starting transfers between devices  119 us (41%)
  other arithmetic  20.3 us (7%)
  local copies, waits for them, and re-layouts  6.11 us (2%)
    ppermute x18, waiting for transfers between devices, padded_2(): after = lax.ppermute(initial, axis, down)  139 us
    ppermute x18, starting transfers between devices, padded_2(): before = lax.ppermute(last, axis, up)  62.5 us
    ppermute x18, starting transfers between devices, padded_2(): after = lax.ppermute(initial, axis, down)  45.1 us
    ppermute x3, starting transfers between devices, shifted(): return lax.ppermute(x, axis, pairs)  11.5 us
    add x3, other arithmetic, sweep_once(): first_state + half_step * (first_rate - slopes[0])  9.95 us
  transfers between devices with their start and end apart: 39, of which 17 were waited for; matrix products, arithmetic and copies ran while one was open for 2% of the time, Pallas kernels for 0%

commit v1 on v0

v1 whole, which is shorter than its diff:
```python
import jax
import jax.numpy as jnp
from jax import lax
from jax.experimental import pallas as pl
from jax.experimental.pallas import tpu as pltpu
from jax.sharding import PartitionSpec as P

MESH = pl.DeviceIdType.MESH
time_step = 0.5
half_step = 0.25
diffusion_low = 0.04
diffusion_high = 0.1
first_weights = (5.0 / 24.0, 1.0 / 3.0, -1.0 / 24.0)
second_weights = (-1.0 / 24.0, 1.0 / 3.0, 5.0 / 24.0)
A = tuple(time_step * w - (half_step if i == 0 else 0.0) for i, w in enumerate(first_weights))
B = tuple(time_step * w - (half_step if i == 1 else 0.0) for i, w in enumerate(second_weights))

BX = 32
BY = 16
ROWS = 2 * BY
X0 = 2
R0 = 16
R1 = R0 + ROWS
FIELDS = 9
XUP, XDOWN, YUP, YDOWN, SHIFT, FORWARD = range(6)


def kernel(shape, start, code, profile, mixing, middle_out, final_out,
           u, h, vm, c1, c2, p1, p2, stage, out_stage, load_sem, store_sem, send_sem, recv_sem):
    nt, nx, ny = shape
    t, gx, gy = (lax.axis_index(a) for a in ("tm", "gx", "gy"))

    loads = []
    for k, source in enumerate((start.at[0], mixing)):
        for half in range(2):
            copy = pltpu.make_async_copy(
                source.at[:, :, pl.ds(128 * half, 128)], stage.at[k, half], load_sem.at[k, half])
            copy.start()
            loads.append(copy)

    def clear(x, carry):
        for l in range(FIELDS):
            u[l, x, pl.ds(R0 - 8, 8), :] = jnp.zeros((8, 128), jnp.float32)
            u[l, x, pl.ds(R1, 8), :] = jnp.zeros((8, 128), jnp.float32)
        return carry

    lax.fori_loop(0, BX + 4, clear, 0)
    for l in range(FIELDS):
        for x in (0, 1, BX + 2, BX + 3):
            u[l, x, pl.ds(R0, ROWS), :] = jnp.zeros((ROWS, 128), jnp.float32)

    later, earlier = (jnp.minimum(t + 1, nt - 1), gx, gy), (jnp.maximum(t - 1, 0), gx, gy)
    has_later, has_earlier = t < nt - 1, t > 0
    neighbours = {
        XUP: (gx < nx - 1, (t, jnp.minimum(gx + 1, nx - 1), gy)),
        XDOWN: (gx > 0, (t, jnp.maximum(gx - 1, 0), gy)),
        YUP: (gy < ny - 1, (t, gx, jnp.minimum(gy + 1, ny - 1))),
        YDOWN: (gy > 0, (t, gx, jnp.maximum(gy - 1, 0))),
    }
    opposite = {XUP: XDOWN, XDOWN: XUP, YUP: YDOWN, YDOWN: YUP}
    far_up, far_down = gy == ny // 2 - 1, gy == ny // 2
    far = far_up | far_down

    barrier = pltpu.get_barrier_semaphore()
    partners = jnp.int32(0)
    for present, device in [*neighbours.values(), (has_later, later), (has_earlier, earlier)]:
        @pl.when(present)
        def _(device=device):
            pl.semaphore_signal(barrier, 1, device_id=device, device_id_type=MESH)
        partners = partners + present.astype(jnp.int32)

    lane = lax.broadcasted_iota(jnp.int32, (ROWS, 128), 1)
    half_of = lax.rem(lax.broadcasted_iota(jnp.int32, (ROWS, 128), 0), 2)
    last_lane, first_lane = lane == 127, lane == 0
    bottom, top = first_lane & (half_of == 0), last_lane & (half_of == 1)
    regime = code[0, 0]
    sign_x = 1 - 2 * lax.rem(regime, 2)
    sign_y = 1 - 2 * lax.rem(regime // 2, 2)
    strength = jnp.where(regime // 4 == 1, diffusion_high, diffusion_low).astype(jnp.float32)
    forward_x = jnp.full((ROWS, 128), sign_x, jnp.int32) > 0
    forward_y = jnp.full((ROWS, 128), sign_y, jnp.int32) > 0

    def wind(i):
        pair = [jnp.broadcast_to(profile[pl.ds(i, 1), pl.ds(128 * k, 128)], (ROWS, 128)) for k in range(2)]
        return 0.5 * jnp.where(half_of == 0, pair[0], pair[1])

    wind_x, wind_y = wind(0), wind(1)
    wind_both = 3.0 * (wind_x + wind_y)

    for copy in loads:
        copy.wait()

    def interleave(x, carry):
        for half in range(2):
            u[0, x + X0, pl.ds(R0 + half, BY, stride=2), :] = stage[0, half, x]
            vm[x, pl.ds(half, BY, stride=2), :] = stage[1, half, x]
        return carry

    lax.fori_loop(0, BX, interleave, 0)
    pl.semaphore_wait(barrier, partners)

    def remote(source, target, l, kind, device):
        return pltpu.make_async_remote_copy(
            src_ref=source, dst_ref=target, send_sem=send_sem.at[l, kind], recv_sem=recv_sem.at[l, kind],
            device_id=device, device_id_type=MESH)

    def edge(l, kind):
        device = neighbours[kind][1]
        own, body = pl.ds(R0, ROWS), pl.ds(X0, BX)
        if kind == XUP:
            return remote(u.at[l, pl.ds(BX, 2), own], u.at[l, pl.ds(0, 2), own], l, kind, device)
        if kind == XDOWN:
            return remote(u.at[l, pl.ds(2, 2), own], u.at[l, pl.ds(BX + 2, 2), own], l, kind, device)
        if kind == YUP:
            return remote(u.at[l, body, pl.ds(R1 - 4, 4)], u.at[l, body, pl.ds(R0 - 4, 4)], l, kind, device)
        return remote(u.at[l, body, pl.ds(R0, 4)], u.at[l, body, pl.ds(R1, 4)], l, kind, device)

    def sends(l, kind):
        ok = neighbours[kind][0]
        if l in (1, 4, 7):
            ok = ok & has_earlier
            if kind == YUP:
                ok = ok & (gy != ny // 2 - 1)
            if kind == YDOWN:
                ok = ok & (gy != ny // 2)
        return ok

    def receives(l, kind):
        ok = neighbours[opposite[kind]][0]
        if l in (1, 4, 7):
            ok = ok & has_earlier
            if kind == YUP:
                ok = ok & (gy != ny // 2)
            if kind == YDOWN:
                ok = ok & (gy != ny // 2 - 1)
        return ok

    def start_edges(l):
        for kind in (YUP, YDOWN, XUP, XDOWN):
            @pl.when(sends(l, kind))
            def _(kind=kind):
                edge(l, kind).start()

    def wait_edges(l):
        for kind in (XUP, XDOWN, YUP, YDOWN):
            @pl.when(receives(l, kind))
            def _(kind=kind):
                edge(l, kind).wait_recv()

    def own(l):
        return u.at[l, pl.ds(X0, BX), pl.ds(R0, ROWS)]

    def shift(l):
        return remote(own(l), own(l + 1), l, SHIFT, later)

    def relay(l):
        row = jnp.where(far_up, R1, R0 - 4)
        part = pl.ds(row, 4)
        return remote(u.at[l, pl.ds(X0, BX), part], u.at[l + 1, pl.ds(X0, BX), part], l, FORWARD, later)

    def start_shift(l):
        @pl.when(has_later)
        def _():
            shift(l).start()

    def start_relay(l):
        @pl.when(has_later & far)
        def _():
            relay(l).start()

    def wait_shift(l):
        @pl.when(has_earlier)
        def _():
            shift(l).wait_recv()

    def wait_relay(l):
        @pl.when(has_earlier & far)
        def _():
            relay(l).wait_recv()

    def tendency(l, write):
        def weights(x, carry):
            v = u[l, x, pl.ds(R0 - 8, ROWS + 16), :]
            h[x, pl.ds(R0 - 8, ROWS + 16), :] = 0.75 - 0.5 / (1.0 + v * v)
            return carry

        lax.fori_loop(1, BX + 3, weights, 0)

        def row(x, carry):
            def at(dx, dr):
                return u[l, x + dx, pl.ds(R0 + dr, ROWS), :]

            def weight(dx, dr):
                return h[x + dx, pl.ds(R0 + dr, ROWS), :]

            c, hc = at(0, 0), weight(0, 0)
            xm, xp, ym, yp = at(-1, 0), at(1, 0), at(0, -2), at(0, 2)
            spread = (hc + weight(1, 0)) * (xp - c) + (hc + weight(-1, 0)) * (xm - c)
            spread = spread + ((hc + weight(0, 2)) * (yp - c) + (hc + weight(0, -2)) * (ym - c))
            near_x = jnp.where(forward_x, xm, xp)
            far_x = jnp.where(forward_x, at(-2, 0), at(2, 0))
            near_y = jnp.where(forward_y, ym, yp)
            far_y = jnp.where(forward_y, at(0, -4), at(0, 4))
            carried = wind_x * (far_x - 4.0 * near_x) + wind_y * (far_y - 4.0 * near_y) + wind_both * c
            below = jnp.where(bottom, c, pltpu.roll(jnp.where(last_lane, at(0, -1), c), 1, axis=1))
            above = jnp.where(top, c, pltpu.roll(jnp.where(first_lane, at(0, 1), c), 127, axis=1))
            rate = strength * spread - carried + vm[x - X0] * (below + above - 2.0 * c)
            write(x, c, rate)
            return carry

        lax.fori_loop(X0, X0 + BX, row, 0)

    def initial(x, c, rate):
        c1[x - X0] = A[0] * rate + A[1] * rate + A[2] * rate
        c2[x - X0] = B[0] * rate + B[1] * rate + B[2] * rate

    def to_middle(l):
        def write(x, c, rate):
            u[l, x, pl.ds(R0, ROWS), :] = c + half_step * rate + c1[x - X0]
            p1[x - X0] = rate
        return write

    def to_final(l):
        def write(x, c, rate):
            u[l, x, pl.ds(R0, ROWS), :] = c + half_step * rate + c2[x - X0]
            g0 = p1[x - X0]
            p1[x - X0] = A[0] * g0 + A[1] * rate
            p2[x - X0] = B[0] * g0 + B[1] * rate
        return write

    def finish(x, c, rate):
        c1[x - X0] = p1[x - X0] + A[2] * rate
        c2[x - X0] = p2[x - X0] + B[2] * rate

    def last(x, c, rate):
        u[0, x, pl.ds(R0, ROWS), :] = c + half_step * rate + c2[x - X0]

    def store(k, l, target):
        def split(x, carry):
            for half in range(2):
                out_stage[k, half, x] = u[l, x + X0, pl.ds(R0 + half, BY, stride=2), :]
            return carry

        lax.fori_loop(0, BX, split, 0)
        copies = [
            pltpu.make_async_copy(out_stage.at[k, half], target.at[0, :, :, pl.ds(128 * half, 128)], store_sem.at[k, half])
            for half in range(2)]
        for copy in copies:
            copy.start()
        return copies

    start_shift(0)
    start_edges(0)
    wait_edges(0)
    start_relay(0)
    tendency(0, initial)
    for sweep in range(3):
        end = 3 * sweep
        first, middle = end + 1, end + 2
        wait_shift(end)
        start_edges(first)
        wait_edges(first)
        wait_relay(end)
        tendency(jnp.where(has_earlier, first, 0), to_middle(middle))
        start_edges(middle)
        if sweep < 2:
            wait_edges(middle)
            tendency(middle, to_final(middle + 1))
            start_shift(middle + 1)
            start_edges(middle + 1)
            wait_edges(middle + 1)
            start_relay(middle + 1)
            tendency(middle + 1, finish)
        else:
            stores = store(0, middle, middle_out)
            wait_edges(middle)
            @pl.when(has_later)
            def _():
                shift(0).wait_send()
            for kind in (XUP, XDOWN, YUP, YDOWN):
                @pl.when(sends(0, kind))
                def _(kind=kind):
                    edge(0, kind).wait_send()
            tendency(middle, last)
            stores += store(1, 0, final_out)

    for l in range(FIELDS):
        for kind in (XUP, XDOWN, YUP, YDOWN):
            if l == 0:
                continue
            @pl.when(sends(l, kind))
            def _(l=l, kind=kind):
                edge(l, kind).wait_send()
    for l in (0, 3, 6):
        if l > 0:
            @pl.when(has_later)
            def _(l=l):
                shift(l).wait_send()
        @pl.when(has_later & far)
        def _(l=l):
            relay(l).wait_send()
    for copy in stores:
        copy.wait()


def solution(mesh):
    shape = tuple(mesh.shape[a] for a in ("tm", "gx", "gy"))

    def shards(start_states, wind_code, wind_profile, vertical_mix):
        block = jax.ShapeDtypeStruct(start_states.shape, jnp.float32)
        field = pltpu.VMEM((BX, ROWS, 128), jnp.float32)
        any_space = pl.BlockSpec(memory_space=pl.ANY)
        return pl.pallas_call(
            lambda *refs: kernel(shape, *refs),
            out_shape=(block, block),
            in_specs=[
                any_space,
                pl.BlockSpec(memory_space=pltpu.SMEM),
                pl.BlockSpec(memory_space=pltpu.VMEM),
                any_space,
            ],
            out_specs=(any_space, any_space),
            scratch_shapes=[
                pltpu.VMEM((FIELDS, BX + 4, ROWS + 32, 128), jnp.float32),
                pltpu.VMEM((BX + 4, ROWS + 32, 128), jnp.float32),
                field, field, field, field, field,
                pltpu.VMEM((2, 2, BX, BY, 128), jnp.float32),
                pltpu.VMEM((2, 2, BX, BY, 128), jnp.float32),
                pltpu.SemaphoreType.DMA((2, 2)),
                pltpu.SemaphoreType.DMA((2, 2)),
                pltpu.SemaphoreType.DMA((FIELDS, 6)),
                pltpu.SemaphoreType.DMA((FIELDS, 6)),
            ],
            compiler_params=pltpu.CompilerParams(
                collective_id=0, has_side_effects=True, vmem_limit_bytes=48 * 1024 * 1024),
        )(start_states, wind_code, wind_profile, vertical_mix)

    in_specs = (P("tm", "gx", "gy", None), P("gx", "gy"), P(), P("gx", "gy", None))
    out_specs = (P("tm", "gx", "gy", None), P("tm", "gx", "gy", None))
    return jax.shard_map(shards, mesh=mesh, in_specs=in_specs, out_specs=out_specs, check_vma=False)
```

time: 288 us -> 127 us (0.44)
  the two profiles are of different devices: /device:TPU:7 before, /device:TPU:79 now
where the time goes in v1:
time: 127 us
  Pallas kernels  121 us (95%)
  local copies, waits for them, and re-layouts  4.35 us (3%)
  between operations  1.29 us (1%)
    pallas_call x1, Pallas kernels, shards(): pl.pallas_call(lambda *refs: kernel(shape, *refs), out_shape=(block, bloc...  121 us
    unnamed x8, local copies, waits for them, and re-layouts  4.35 us

profile of v1, /device:TPU:79, one launch (start us, length us, event | category | flops | bytes accessed | tf_op | source)
XLA Modules:
  0.0 126.8 jit_solution(8605063119379589276)
XLA Ops:
  1.3 0.0 copy-start
  1.3 1.0 copy-done
  2.3 0.0 copy-start.1
  2.3 1.0 copy-done.1
  3.4 0.0 copy-start.2
  3.4 0.7 copy-done.2
  4.0 121.1 %shard_map.59 = (f32[1,32,16,256]{3,2,1,0:T(8,128)S(1)}, f32[1,32,16,256]{3,2,1,0:T(8,128)S(1)}) custom-call(f32[1,32,16,256]{3,2,1,0:T(8,128)S(1)} %copy-done, s32[1,1]{1,0:T(1,128)S(6)} %copy.8.refs_1_, f32[2,256]{1,0:T(2,128)S(1)} %copy-done.2, f32[32,16,256]{2,1,0:T(8,128)S(1)} %copy-done.1), custom_call_target="tpu_custom_call" | custom-call | tf_op jit(solution)/shard_map/pallas_call | solution.py:313
  125.2 0.8 copy.9
  126.0 0.8 copy.10
Async XLA Ops:
  1.3 1.0 copy-start
  2.3 1.0 copy-start.1
  3.4 0.7 copy-start.2

commit v2 on v1

v2 whole, which is shorter than its diff:
```python
import jax
import jax.numpy as jnp
from jax import lax
from jax.experimental import pallas as pl
from jax.experimental.pallas import tpu as pltpu
from jax.sharding import PartitionSpec as P

MESH = pl.DeviceIdType.MESH
time_step = 0.5
half_step = 0.25
diffusion_low = 0.04
diffusion_high = 0.1
first_weights = (5.0 / 24.0, 1.0 / 3.0, -1.0 / 24.0)
second_weights = (-1.0 / 24.0, 1.0 / 3.0, 5.0 / 24.0)
A = tuple(time_step * w - (half_step if i == 0 else 0.0) for i, w in enumerate(first_weights))
B = tuple(time_step * w - (half_step if i == 1 else 0.0) for i, w in enumerate(second_weights))

BX = 32
BY = 16
ROWS = 2 * BY
X0 = 2
R0 = 16
R1 = R0 + ROWS
FIELDS = 9
XUP, XDOWN, YUP, YDOWN, SHIFT, REST = range(6)
NEXT = 6


def kernel(shape, start, code, profile, mixing, middle_out, final_out,
           u, h, vm, c1, c2, p1, p2, border, border_c, stage, out_stage, load_sem, store_sem, send_sem, recv_sem):
    nt, nx, ny = shape
    t, gx, gy = (lax.axis_index(a) for a in ("tm", "gx", "gy"))

    loads = []
    for k, source in enumerate((start.at[0], mixing)):
        for half in range(2):
            copy = pltpu.make_async_copy(
                source.at[:, :, pl.ds(128 * half, 128)], stage.at[k, half], load_sem.at[k, half])
            copy.start()
            loads.append(copy)

    def clear(x, carry):
        for l in range(FIELDS):
            u[l, x, pl.ds(R0 - 8, 8), :] = jnp.zeros((8, 128), jnp.float32)
            u[l, x, pl.ds(R1, 8), :] = jnp.zeros((8, 128), jnp.float32)
        return carry

    lax.fori_loop(0, BX + 4, clear, 0)
    for l in range(FIELDS):
        for x in (0, 1, BX + 2, BX + 3):
            u[l, x, pl.ds(R0, ROWS), :] = jnp.zeros((ROWS, 128), jnp.float32)

    later, earlier = (jnp.minimum(t + 1, nt - 1), gx, gy), (jnp.maximum(t - 1, 0), gx, gy)
    has_later, has_earlier = t < nt - 1, t > 0
    neighbours = {
        XUP: (gx < nx - 1, (t, jnp.minimum(gx + 1, nx - 1), gy)),
        XDOWN: (gx > 0, (t, jnp.maximum(gx - 1, 0), gy)),
        YUP: (gy < ny - 1, (t, gx, jnp.minimum(gy + 1, ny - 1))),
        YDOWN: (gy > 0, (t, gx, jnp.maximum(gy - 1, 0))),
    }
    opposite = {XUP: XDOWN, XDOWN: XUP, YUP: YDOWN, YDOWN: YUP}
    far_up, far_down = gy == ny // 2 - 1, gy == ny // 2
    far = far_up | far_down

    def at_time(device, step):
        return (jnp.clip(t + step, 0, nt - 1), device[1], device[2])

    barrier = pltpu.get_barrier_semaphore()
    partners = jnp.int32(0)
    pairs = [(has_later, later), (has_earlier, earlier)]
    for present, device in neighbours.values():
        pairs += [(present, device), (present & has_later, at_time(device, 1)), (present & has_earlier, at_time(device, -1))]
    for present, device in pairs:
        @pl.when(present)
        def _(device=device):
            pl.semaphore_signal(barrier, 1, device_id=device, device_id_type=MESH)
        partners = partners + present.astype(jnp.int32)

    regime = code[0, 0]
    sign_x = 1 - 2 * lax.rem(regime, 2)
    sign_y = 1 - 2 * lax.rem(regime // 2, 2)
    strength = jnp.where(regime // 4 == 1, diffusion_high, diffusion_low).astype(jnp.float32)

    def constants(rows):
        lane = lax.broadcasted_iota(jnp.int32, (rows, 128), 1)
        half_of = lax.rem(lax.broadcasted_iota(jnp.int32, (rows, 128), 0), 2)

        def wind(i):
            pair = [jnp.broadcast_to(profile[pl.ds(i, 1), pl.ds(128 * k, 128)], (rows, 128)) for k in range(2)]
            return 0.5 * jnp.where(half_of == 0, pair[0], pair[1])

        wind_x, wind_y = wind(0), wind(1)
        return (
            lane == 127, lane == 0, (lane == 0) & (half_of == 0), (lane == 127) & (half_of == 1),
            jnp.full((rows, 128), sign_x, jnp.int32) > 0, jnp.full((rows, 128), sign_y, jnp.int32) > 0,
            wind_x, wind_y, 3.0 * (wind_x + wind_y))

    for copy in loads:
        copy.wait()

    def interleave(x, carry):
        for half in range(2):
            u[0, x + X0, pl.ds(R0 + half, BY, stride=2), :] = stage[0, half, x]
            vm[x, pl.ds(half, BY, stride=2), :] = stage[1, half, x]
        return carry

    lax.fori_loop(0, BX, interleave, 0)
    pl.semaphore_wait(barrier, partners)

    def remote(source, target, l, kind, device):
        return pltpu.make_async_remote_copy(
            src_ref=source, dst_ref=target, send_sem=send_sem.at[l, kind], recv_sem=recv_sem.at[l, kind],
            device_id=device, device_id_type=MESH)

    def edge(l, kind, step=0, source=None):
        device = at_time(neighbours[kind][1], step)
        m = l + step
        own, body = pl.ds(R0, ROWS), pl.ds(X0, BX)
        if kind == XUP:
            source, target = u.at[l, pl.ds(BX, 2), own], u.at[m, pl.ds(0, 2), own]
        elif kind == XDOWN:
            source, target = u.at[l, pl.ds(2, 2), own], u.at[m, pl.ds(BX + 2, 2), own]
        elif kind == YUP:
            source, target = source or u.at[l, body, pl.ds(R1 - 4, 4)], u.at[m, body, pl.ds(R0 - 4, 4)]
        else:
            source, target = source or u.at[l, body, pl.ds(R0, 4)], u.at[m, body, pl.ds(R1, 4)]
        return remote(source, target, l, kind + NEXT * step, device)

    def is_far(kind, receiving=False):
        if kind in (XUP, XDOWN):
            return None
        return far_up if (kind == YUP) != receiving else far_down

    def each_edge(action, l, kinds=(YUP, YDOWN, XUP, XDOWN), step=0, far_ones=None):
        receiving = action == "wait_recv"
        for kind in kinds:
            ok = neighbours[opposite[kind] if receiving else kind][0]
            if step:
                ok = ok & (has_earlier if receiving else has_later)
            crossing = is_far(kind, receiving)
            if far_ones is not None:
                if crossing is None:
                    continue
                ok = ok & (crossing if far_ones else ~crossing)

            @pl.when(ok)
            def _(kind=kind):
                source = border.at[l // 3] if far_ones and l % 3 == 2 else None
                getattr(edge(l, kind, step, source), action)()

    def shift(l, kind):
        if kind == SHIFT:
            rows = pl.ds(jnp.where(far_up, R1 - 8, R0), 8)
        else:
            rows = pl.ds(jnp.where(far_up, R0, R0 + 8), ROWS - 8)
        body = pl.ds(X0, BX)
        return remote(u.at[l, body, rows], u.at[l + 1, body, rows], l, kind, later)

    def each_shift(action, l, kind):
        @pl.when(has_earlier if action == "wait_recv" else has_later)
        def _():
            getattr(shift(l, kind), action)()

    def tendency(l, write, r0=R0, rows=ROWS, parts=((X0, X0 + BX, None),), unroll=4):
        last_lane, first_lane, bottom, top, forward_x, forward_y, wind_x, wind_y, wind_both = constants(rows)

        def weights(x, carry):
            v = u[l, x, pl.ds(r0 - 2, rows + 4), :]
            h[x, pl.ds(r0 - 2, rows + 4), :] = 0.75 - 0.5 / (1.0 + v * v)
            return carry

        lax.fori_loop(1, BX + 3, weights, 0, unroll=2)

        def row(x, carry):
            def at(dx, dr):
                return u[l, x + dx, pl.ds(r0 + dr, rows), :]

            def weight(dx, dr):
                return h[x + dx, pl.ds(r0 + dr, rows), :]

            c, hc = at(0, 0), weight(0, 0)
            xm, xp, ym, yp = at(-1, 0), at(1, 0), at(0, -2), at(0, 2)
            spread = (hc + weight(1, 0)) * (xp - c) + (hc + weight(-1, 0)) * (xm - c)
            spread = spread + ((hc + weight(0, 2)) * (yp - c) + (hc + weight(0, -2)) * (ym - c))
            near_x = jnp.where(forward_x, xm, xp)
            far_x = jnp.where(forward_x, at(-2, 0), at(2, 0))
            near_y = jnp.where(forward_y, ym, yp)
            far_y = jnp.where(forward_y, at(0, -4), at(0, 4))
            carried = wind_x * (far_x - 4.0 * near_x) + wind_y * (far_y - 4.0 * near_y) + wind_both * c
            below = jnp.where(bottom, c, pltpu.roll(jnp.where(last_lane, at(0, -1), c), 1, axis=1))
            above = jnp.where(top, c, pltpu.roll(jnp.where(first_lane, at(0, 1), c), 127, axis=1))
            rate = strength * spread - carried + vm[x - X0, pl.ds(r0 - R0, rows), :] * (below + above - 2.0 * c)
            write(x, c, rate)
            return carry

        for begin, end, after in parts:
            lax.fori_loop(begin, end, row, 0, unroll=min(unroll, end - begin))
            if after is not None:
                after()

    def initial(x, c, rate):
        c1[x - X0] = A[0] * rate + A[1] * rate + A[2] * rate
        c2[x - X0] = B[0] * rate + B[1] * rate + B[2] * rate

    def to_middle(l):
        def write(x, c, rate):
            u[l, x, pl.ds(R0, ROWS), :] = c + half_step * rate + c1[x - X0]
            p1[x - X0] = rate
        return write

    def to_final(l):
        def write(x, c, rate):
            u[l, x, pl.ds(R0, ROWS), :] = c + half_step * rate + c2[x - X0]
            g0 = p1[x - X0]
            p1[x - X0] = A[0] * g0 + A[1] * rate
            p2[x - X0] = B[0] * g0 + B[1] * rate
        return write

    def finish(x, c, rate):
        c1[x - X0] = p1[x - X0] + A[2] * rate
        c2[x - X0] = p2[x - X0] + B[2] * rate

    def last(x, c, rate):
        u[0, x, pl.ds(R0, ROWS), :] = c + half_step * rate + c2[x - X0]

    def store(k, l, target):
        def split(x, carry):
            for half in range(2):
                out_stage[k, half, x] = u[l, x + X0, pl.ds(R0 + half, BY, stride=2), :]
            return carry

        lax.fori_loop(0, BX, split, 0)
        copies = [
            pltpu.make_async_copy(out_stage.at[k, half], target.at[0, :, :, pl.ds(128 * half, 128)], store_sem.at[k, half])
            for half in range(2)]
        for copy in copies:
            copy.start()
        return copies

    def border_first(sweep, end, source):
        def run(r0, kind):
            rows = pl.ds(r0 - R0, 4)

            def slopes(x, c, rate):
                if sweep == 0:
                    border_c[x - X0] = A[0] * rate + A[1] * rate + A[2] * rate
                else:
                    border_c[x - X0] = p1[x - X0, rows, :] + A[2] * rate

            def state(x, c, rate):
                border[sweep, x - X0] = c + half_step * rate + border_c[x - X0]

            each_edge("wait_recv", end, (opposite[kind],))
            tendency(end, slopes, r0, 4, unroll=8)
            each_shift("wait_recv", end, SHIFT)
            each_edge("wait_recv", end, (XUP, XDOWN, opposite[kind]), step=1)
            tendency(source, state, r0, 4, unroll=8)

        each_edge("wait_recv", end, (XUP, XDOWN))

        @pl.when(far_up)
        def _():
            run(R1 - 4, YUP)

        @pl.when(far_down)
        def _():
            run(R0, YDOWN)

    stores = []
    for sweep in range(3):
        end, middle = 3 * sweep, 3 * sweep + 2
        source = jnp.where(has_earlier, end + 1, 0)
        each_edge("start", end, (YUP, YDOWN), far_ones=True)
        each_edge("start", end, (YUP, YDOWN), step=1, far_ones=True)
        each_edge("start", end, (XUP, XDOWN))
        each_edge("start", end, (YUP, YDOWN), far_ones=False)
        each_shift("start", end, SHIFT)
        each_edge("start", end, (XUP, XDOWN), step=1)
        each_edge("start", end, (YUP, YDOWN), step=1, far_ones=False)
        each_shift("start", end, REST)
        border_first(sweep, end, source)
        each_edge("start", middle, (YUP, YDOWN), far_ones=True)
        each_edge("wait_recv", end, (YUP, YDOWN), far_ones=False)
        tendency(end, initial if sweep == 0 else finish)

        @pl.when(~far)
        def _():
            each_shift("wait_recv", end, SHIFT)
            each_edge("wait_recv", end, (XUP, XDOWN), step=1)

        each_edge("wait_recv", end, (YUP, YDOWN), step=1, far_ones=False)
        each_shift("wait_recv", end, REST)

        def send_x():
            each_edge("start", middle, (XUP, XDOWN))

        tendency(source, to_middle(middle), parts=(
            (X0, X0 + 2, None), (X0 + BX - 2, X0 + BX, send_x), (X0 + 2, X0 + BX - 2, None)))
        each_edge("start", middle, (YUP, YDOWN), far_ones=False)
        if sweep == 2:
            stores += store(0, middle, middle_out)
        each_edge("wait_recv", middle)
        if sweep < 2:
            tendency(middle, to_final(middle + 1))
        else:
            each_edge("wait_send", 0)
            each_edge("wait_send", 0, step=1)
            each_shift("wait_send", 0, SHIFT)
            each_shift("wait_send", 0, REST)
            tendency(middle, last)
            stores += store(1, 0, final_out)

    for end in (0, 3, 6):
        if end:
            each_edge("wait_send", end)
            each_edge("wait_send", end, step=1)
            each_shift("wait_send", end, SHIFT)
            each_shift("wait_send", end, REST)
        each_edge("wait_send", end + 2, (XUP, XDOWN))
        each_edge("wait_send", end + 2, (YUP, YDOWN), far_ones=False)
        each_edge("wait_send", end + 2, (YUP, YDOWN), far_ones=True)
    for copy in stores:
        copy.wait()


def solution(mesh):
    shape = tuple(mesh.shape[a] for a in ("tm", "gx", "gy"))

    def shards(start_states, wind_code, wind_profile, vertical_mix):
        block = jax.ShapeDtypeStruct(start_states.shape, jnp.float32)
        field = pltpu.VMEM((BX, ROWS, 128), jnp.float32)
        any_space = pl.BlockSpec(memory_space=pl.ANY)
        return pl.pallas_call(
            lambda *refs: kernel(shape, *refs),
            out_shape=(block, block),
            in_specs=[
                any_space,
                pl.BlockSpec(memory_space=pltpu.SMEM),
                pl.BlockSpec(memory_space=pltpu.VMEM),
                any_space,
            ],
            out_specs=(any_space, any_space),
            scratch_shapes=[
                pltpu.VMEM((FIELDS, BX + 4, ROWS + 32, 128), jnp.float32),
                pltpu.VMEM((BX + 4, ROWS + 32, 128), jnp.float32),
                field, field, field, field, field,
                pltpu.VMEM((3, BX, 4, 128), jnp.float32),
                pltpu.VMEM((BX, 4, 128), jnp.float32),
                pltpu.VMEM((2, 2, BX, BY, 128), jnp.float32),
                pltpu.VMEM((2, 2, BX, BY, 128), jnp.float32),
                pltpu.SemaphoreType.DMA((2, 2)),
                pltpu.SemaphoreType.DMA((2, 2)),
                pltpu.SemaphoreType.DMA((FIELDS, 2 * NEXT)),
                pltpu.SemaphoreType.DMA((FIELDS, 2 * NEXT)),
            ],
            compiler_params=pltpu.CompilerParams(
                collective_id=0, has_side_effects=True),
        )(start_states, wind_code, wind_profile, vertical_mix)

    in_specs = (P("tm", "gx", "gy", None), P("gx", "gy"), P(), P("gx", "gy", None))
    out_specs = (P("tm", "gx", "gy", None), P("tm", "gx", "gy", None))
    return jax.shard_map(shards, mesh=mesh, in_specs=in_specs, out_specs=out_specs, check_vma=False)
```

time: 127 us -> 92 us (0.72)
  the two profiles are of different devices: /device:TPU:79 before, /device:TPU:89 now
where the time goes in v2:
time: 92 us; the launch traced here: 91.8 us
  Pallas kernels  87.8 us (95%)
  local copies, waits for them, and re-layouts  2.72 us (3%)
  between operations  1.29 us (1%)
    pallas_call x1, Pallas kernels, shards(): pl.pallas_call(lambda *refs: kernel(shape, *refs), out_shape=(block, bloc...  87.8 us
    unnamed x4, local copies, waits for them, and re-layouts  2.72 us

profile of v2, /device:TPU:89, one launch (start us, length us, event | category | flops | bytes accessed | tf_op | source)
XLA Modules:
  0.0 91.8 jit_solution(10645460069059521879)
XLA Ops:
  1.3 87.8 %shard_map.59 = (f32[1,32,16,256]{3,2,1,0:T(8,128)}, f32[1,32,16,256]{3,2,1,0:T(8,128)}) custom-call(f32[1,32,16,256]{3,2,1,0:T(8,128)} %refs_0_.1, s32[1,1]{1,0:T(1,128)S(6)} %copy.8.refs_1_, f32[2,256]{1,0:T(2,128)} %refs_2_.1, f32[32,16,256]{2,1,0:T(8,128)} %refs_3_.1), custom_call_target="tpu_custom_call" | custom-call | tf_op jit(solution)/shard_map/pallas_call | solution.py:333
  89.1 0.0 copy-start
  89.1 1.9 %copy.9 = f32[1,32,16,256]{3,2,1,0:T(8,128)} copy(f32[1,32,16,256]{3,2,1,0:T(8,128)} %get-tuple-element.4) | data formatting | bytes 1048576
  91.0 0.0 copy-done
  91.0 0.8 copy.10
Async XLA Ops:
  89.1 1.9 %copy-start = (f32[1,32,16,256]{3,2,1,0:T(8,128)S(1)}, f32[1,32,16,256]{3,2,1,0:T(8,128)}, u32[]{:S(2)}) copy-start(f32[1,32,16,256]{3,2,1,0:T(8,128)} %get-tuple-element.5) | copy-start | bytes 1572868

commit v3 on v2

--- a/solution.py
+++ b/solution.py
@@ -22,16 +22,17 @@
 R0 = 16
 R1 = R0 + ROWS
 FIELDS = 9
-XUP, XDOWN, YUP, YDOWN, SHIFT, REST = range(6)
-NEXT = 6
-
-
-def kernel(shape, start, code, profile, mixing, middle_out, final_out,
-           u, h, vm, c1, c2, p1, p2, border, border_c, stage, out_stage, load_sem, store_sem, send_sem, recv_sem):
+XUP, XDOWN, YUP, YDOWN, STRIP, LOW, HIGH, REST = range(8)
+NEXT = 8
+
+
+def kernel(shape, start, code, wind_profile, mixing, middle_out, final_out,
+           u, h, vm, c1, c2, p1, p2, border, border_c, stage, profile, profile_sem, load_sem, send_sem, recv_sem):
     nt, nx, ny = shape
     t, gx, gy = (lax.axis_index(a) for a in ("tm", "gx", "gy"))
 
-    loads = []
+    loads = [pltpu.make_async_copy(wind_profile, profile, profile_sem)]
+    loads[0].start()
     for k, source in enumerate((start.at[0], mixing)):
         for half in range(2):
             copy = pltpu.make_async_copy(
@@ -149,11 +150,11 @@
                 getattr(edge(l, kind, step, source), action)()
 
     def shift(l, kind):
-        if kind == SHIFT:
-            rows = pl.ds(jnp.where(far_up, R1 - 8, R0), 8)
+        if kind == STRIP:
+            rows, body = pl.ds(jnp.where(far_up, R1 - 8, R0), 8), pl.ds(X0, BX)
         else:
             rows = pl.ds(jnp.where(far_up, R0, R0 + 8), ROWS - 8)
-        body = pl.ds(X0, BX)
+            body = {LOW: pl.ds(X0, 4), HIGH: pl.ds(X0 + BX - 4, 4), REST: pl.ds(X0 + 4, BX - 8)}[kind]
         return remote(u.at[l, body, rows], u.at[l + 1, body, rows], l, kind, later)
 
     def each_shift(action, l, kind):
@@ -161,15 +162,13 @@
         def _():
             getattr(shift(l, kind), action)()
 
-    def tendency(l, write, r0=R0, rows=ROWS, parts=((X0, X0 + BX, None),), unroll=4):
+    def tendency(l, write, r0=R0, rows=ROWS, begin=X0, end=X0 + BX, unroll=4):
         last_lane, first_lane, bottom, top, forward_x, forward_y, wind_x, wind_y, wind_both = constants(rows)
 
         def weights(x, carry):
             v = u[l, x, pl.ds(r0 - 2, rows + 4), :]
             h[x, pl.ds(r0 - 2, rows + 4), :] = 0.75 - 0.5 / (1.0 + v * v)
             return carry
-
-        lax.fori_loop(1, BX + 3, weights, 0, unroll=2)
 
         def row(x, carry):
             def at(dx, dr):
@@ -193,51 +192,62 @@
             write(x, c, rate)
             return carry
 
-        for begin, end, after in parts:
-            lax.fori_loop(begin, end, row, 0, unroll=min(unroll, end - begin))
-            if after is not None:
-                after()
+        if begin is None:
+            for x in (1, 2, 3, 4, BX - 1, BX, BX + 1, BX + 2):
+                weights(x, 0)
+            for x in (X0, X0 + 1, BX, BX + 1):
+                row(x, 0)
+        else:
+            lax.fori_loop(begin - 1, end + 1, weights, 0, unroll=2)
+            lax.fori_loop(begin, end, row, 0, unroll=unroll)
 
     def initial(x, c, rate):
         c1[x - X0] = A[0] * rate + A[1] * rate + A[2] * rate
         c2[x - X0] = B[0] * rate + B[1] * rate + B[2] * rate
 
-    def to_middle(l):
+    def to_middle(l, out):
         def write(x, c, rate):
-            u[l, x, pl.ds(R0, ROWS), :] = c + half_step * rate + c1[x - X0]
-            p1[x - X0] = rate
+            state = c + half_step * rate + c1[x - X0]
+            u[l, x, pl.ds(R0, ROWS), :] = state
+            if out is None:
+                p1[x - X0] = rate
+            else:
+                out[x - X0] = state
         return write
 
-    def to_final(l):
+    def to_final(l, r0, rows):
+        own = pl.ds(r0 - R0, rows)
+
         def write(x, c, rate):
-            u[l, x, pl.ds(R0, ROWS), :] = c + half_step * rate + c2[x - X0]
-            g0 = p1[x - X0]
-            p1[x - X0] = A[0] * g0 + A[1] * rate
-            p2[x - X0] = B[0] * g0 + B[1] * rate
+            u[l, x, pl.ds(r0, rows), :] = c + half_step * rate + c2[x - X0, own, :]
+            g0 = p1[x - X0, own, :]
+            p1[x - X0, own, :] = A[0] * g0 + A[1] * rate
+            p2[x - X0, own, :] = B[0] * g0 + B[1] * rate
         return write
 
     def finish(x, c, rate):
         c1[x - X0] = p1[x - X0] + A[2] * rate
         c2[x - X0] = p2[x - X0] + B[2] * rate
 
-    def last(x, c, rate):
-        u[0, x, pl.ds(R0, ROWS), :] = c + half_step * rate + c2[x - X0]
-
-    def store(k, l, target):
-        def split(x, carry):
-            for half in range(2):
-                out_stage[k, half, x] = u[l, x + X0, pl.ds(R0 + half, BY, stride=2), :]
+    def last(r0, rows):
+        own = pl.ds(r0 - R0, rows)
+
+        def write(x, c, rate):
+            final_out[x - X0, own, :] = c + half_step * rate + c2[x - X0, own, :]
+        return write
+
+    def copy_start():
+        def body(x, carry):
+            rows = pl.ds(R0 - 8, ROWS + 16)
+            for l in (1, 4, 7):
+                u[l, x, rows, :] = u[0, x, rows, :]
             return carry
 
-        lax.fori_loop(0, BX, split, 0)
-        copies = [
-            pltpu.make_async_copy(out_stage.at[k, half], target.at[0, :, :, pl.ds(128 * half, 128)], store_sem.at[k, half])
-            for half in range(2)]
-        for copy in copies:
-            copy.start()
-        return copies
-
-    def border_first(sweep, end, source):
+        @pl.when(~has_earlier)
+        def _():
+            lax.fori_loop(0, BX + 4, body, 0, unroll=2)
+
+    def border_first(sweep, end):
         def run(r0, kind):
             rows = pl.ds(r0 - R0, 4)
 
@@ -252,11 +262,13 @@
 
             each_edge("wait_recv", end, (opposite[kind],))
             tendency(end, slopes, r0, 4, unroll=8)
-            each_shift("wait_recv", end, SHIFT)
+            if sweep == 0:
+                copy_start()
+            each_shift("wait_recv", end, STRIP)
             each_edge("wait_recv", end, (XUP, XDOWN, opposite[kind]), step=1)
-            tendency(source, state, r0, 4, unroll=8)
-
-        each_edge("wait_recv", end, (XUP, XDOWN))
+            tendency(end + 1, state, r0, 4, unroll=8)
+
+        each_edge("wait_recv", end, (YUP, YDOWN), far_ones=False)
 
         @pl.when(far_up)
         def _():
@@ -266,61 +278,82 @@
         def _():
             run(R0, YDOWN)
 
-    stores = []
+        if sweep == 0:
+            @pl.when(~far)
+            def _():
+                copy_start()
+
     for sweep in range(3):
-        end, middle = 3 * sweep, 3 * sweep + 2
-        source = jnp.where(has_earlier, end + 1, 0)
+        end, first, middle = 3 * sweep, 3 * sweep + 1, 3 * sweep + 2
         each_edge("start", end, (YUP, YDOWN), far_ones=True)
         each_edge("start", end, (YUP, YDOWN), step=1, far_ones=True)
+        each_edge("start", end, (XUP, XDOWN), step=1)
         each_edge("start", end, (XUP, XDOWN))
         each_edge("start", end, (YUP, YDOWN), far_ones=False)
-        each_shift("start", end, SHIFT)
-        each_edge("start", end, (XUP, XDOWN), step=1)
+        each_shift("start", end, STRIP)
         each_edge("start", end, (YUP, YDOWN), step=1, far_ones=False)
-        each_shift("start", end, REST)
-        border_first(sweep, end, source)
+        each_edge("wait_recv", end, (XUP, XDOWN))
+        for kind in (LOW, HIGH, REST):
+            each_shift("start", end, kind)
+        border_first(sweep, end)
         each_edge("start", middle, (YUP, YDOWN), far_ones=True)
-        each_edge("wait_recv", end, (YUP, YDOWN), far_ones=False)
         tendency(end, initial if sweep == 0 else finish)
 
         @pl.when(~far)
         def _():
-            each_shift("wait_recv", end, SHIFT)
+            each_shift("wait_recv", end, STRIP)
             each_edge("wait_recv", end, (XUP, XDOWN), step=1)
 
         each_edge("wait_recv", end, (YUP, YDOWN), step=1, far_ones=False)
+        each_shift("wait_recv", end, LOW)
+        each_shift("wait_recv", end, HIGH)
+        write = to_middle(middle, middle_out if sweep == 2 else None)
+        tendency(first, write, begin=None)
+        each_edge("start", middle, (XUP, XDOWN))
         each_shift("wait_recv", end, REST)
-
-        def send_x():
-            each_edge("start", middle, (XUP, XDOWN))
-
-        tendency(source, to_middle(middle), parts=(
-            (X0, X0 + 2, None), (X0 + BX - 2, X0 + BX, send_x), (X0 + 2, X0 + BX - 2, None)))
+        tendency(first, write, begin=X0 + 2, end=X0 + BX - 2)
         each_edge("start", middle, (YUP, YDOWN), far_ones=False)
-        if sweep == 2:
-            stores += store(0, middle, middle_out)
-        each_edge("wait_recv", middle)
-        if sweep < 2:
-            tendency(middle, to_final(middle + 1))
-        else:
-            each_edge("wait_send", 0)
-            each_edge("wait_send", 0, step=1)
-            each_shift("wait_send", 0, SHIFT)
-            each_shift("wait_send", 0, REST)
-            tendency(middle, last)
-            stores += store(1, 0, final_out)
+        each_edge("wait_recv", middle, (XUP, XDOWN))
+        each_edge("wait_recv", middle, (YUP, YDOWN), far_ones=False)
+
+        def part(r0, rows, unroll=4):
+            write = to_final(middle + 1, r0, rows) if sweep < 2 else last(r0, rows)
+            tendency(middle, write, r0, rows, unroll=unroll)
+
+        @pl.when(~far)
+        def _():
+            part(R0, ROWS)
+
+        @pl.when(far_up)
+        def _():
+            part(R0, ROWS - 4)
+            each_edge("wait_recv", middle, (YDOWN,))
+            part(R1 - 4, 4, 8)
+
+        @pl.when(far_down)
+        def _():
+            part(R0 + 4, ROWS - 4)
+            each_edge("wait_recv", middle, (YUP,))
+            part(R0, 4, 8)
 
     for end in (0, 3, 6):
-        if end:
-            each_edge("wait_send", end)
-            each_edge("wait_send", end, step=1)
-            each_shift("wait_send", end, SHIFT)
-            each_shift("wait_send", end, REST)
+        each_edge("wait_send", end)
+        each_edge("wait_send", end, step=1)
+        for kind in (STRIP, LOW, HIGH, REST):
+            each_shift("wait_send", end, kind)
         each_edge("wait_send", end + 2, (XUP, XDOWN))
         each_edge("wait_send", end + 2, (YUP, YDOWN), far_ones=False)
         each_edge("wait_send", end + 2, (YUP, YDOWN), far_ones=True)
-    for copy in stores:
-        copy.wait()
+
+
+def unpack(middle, final, middle_out, final_out):
+    def body(x, carry):
+        for source, target in ((middle, middle_out), (final, final_out)):
+            for half in range(2):
+                target[0, x, :, pl.ds(128 * half, 128)] = source[x, pl.ds(half, BY, stride=2), :]
+        return carry
+
+    lax.fori_loop(0, middle.shape[0], body, 0, unroll=4)
 
 
 def solution(mesh):
@@ -328,18 +361,14 @@
 
     def shards(start_states, wind_code, wind_profile, vertical_mix):
         block = jax.ShapeDtypeStruct(start_states.shape, jnp.float32)
-        field = pltpu.VMEM((BX, ROWS, 128), jnp.float32)
-        any_space = pl.BlockSpec(memory_space=pl.ANY)
-        return pl.pallas_call(
+        packed = jax.ShapeDtypeStruct((BX, ROWS, 128), jnp.float32)
+        field = pltpu.VMEM(packed.shape, jnp.float32)
+        any_space, vmem = pl.BlockSpec(memory_space=pl.ANY), pl.BlockSpec(memory_space=pltpu.VMEM)
+        middle, final = pl.pallas_call(
             lambda *refs: kernel(shape, *refs),
-            out_shape=(block, block),
-            in_specs=[
-                any_space,
-                pl.BlockSpec(memory_space=pltpu.SMEM),
-                pl.BlockSpec(memory_space=pltpu.VMEM),
-                any_space,
-            ],
-            out_specs=(any_space, any_space),
+            out_shape=(packed, packed),
+            in_specs=[any_space, pl.BlockSpec(memory_space=pltpu.SMEM), any_space, any_space],
+            out_specs=(vmem, vmem),
             scratch_shapes=[
                 pltpu.VMEM((FIELDS, BX + 4, ROWS + 32, 128), jnp.float32),
                 pltpu.VMEM((BX + 4, ROWS + 32, 128), jnp.float32),
@@ -347,15 +376,21 @@
                 pltpu.VMEM((3, BX, 4, 128), jnp.float32),
                 pltpu.VMEM((BX, 4, 128), jnp.float32),
                 pltpu.VMEM((2, 2, BX, BY, 128), jnp.float32),
-                pltpu.VMEM((2, 2, BX, BY, 128), jnp.float32),
+                pltpu.VMEM((2, 256), jnp.float32),
+                pltpu.SemaphoreType.DMA,
                 pltpu.SemaphoreType.DMA((2, 2)),
-                pltpu.SemaphoreType.DMA((2, 2)),
-                pltpu.SemaphoreType.DMA((FIELDS, 2 * NEXT)),
-                pltpu.SemaphoreType.DMA((FIELDS, 2 * NEXT)),
+                pltpu.SemaphoreType.DMA((FIELDS, NEXT + 4)),
+                pltpu.SemaphoreType.DMA((FIELDS, NEXT + 4)),
             ],
-            compiler_params=pltpu.CompilerParams(
-                collective_id=0, has_side_effects=True),
-        )(start_states, wind_code, wind_profile, vertical_mix)
+            compiler_params=pltpu.CompilerParams(collective_id=0, has_side_effects=True, vmem_limit_bytes=54000 * 1024),
+        )(start_states, wind_code, pltpu.with_memory_space_constraint(wind_profile, pltpu.HBM), vertical_mix)
+        return pl.pallas_call(
+            unpack,
+            out_shape=(block, block),
+            in_specs=[vmem, vmem],
+            out_specs=(vmem, vmem),
+            compiler_params=pltpu.CompilerParams(vmem_limit_bytes=8 * 1024 * 1024),
+        )(middle, final)
 
     in_specs = (P("tm", "gx", "gy", None), P("gx", "gy"), P(), P("gx", "gy", None))
     out_specs = (P("tm", "gx", "gy", None), P("tm", "gx", "gy", None))

time: 92 us -> 85.9 us (0.934)
  Pallas kernels: 87.8 us -> 84.5 us
  local copies, waits for them, and re-layouts: 2.72 us -> 0 us
    pallas_call x1 -> x2, Pallas kernels: 87.8 us -> 84.5 us  [the longest x1 83.4 us: shards(): pl.pallas_call(lambda *refs: kernel(shape, *refs), out_shape=(packed, pac...]
    unnamed x4 -> x0, local copies, waits for them, and re-layouts: 2.72 us -> none
where the time goes in v3:
time: 85.9 us; the launch traced here: 85.8 us
  Pallas kernels  84.5 us (98%)
  between operations  1.28 us (1%)
    pallas_call x1, Pallas kernels, shards(): pl.pallas_call(lambda *refs: kernel(shape, *refs), out_shape=(packed, pac...  83.4 us

profile of v3, /device:TPU:89, one launch (start us, length us, event | category | flops | bytes accessed | tf_op | source)
XLA Modules:
  0.0 85.8 jit_solution(17214767377681416398)
XLA Ops:
  1.3 83.4 %shard_map.59 = (f32[32,32,128]{2,1,0:T(8,128)S(1)}, f32[32,32,128]{2,1,0:T(8,128)S(1)}) custom-call(f32[1,32,16,256]{3,2,1,0:T(8,128)} %refs_0_.1, s32[1,1]{1,0:T(1,128)S(6)} %copy.6.refs_1_, f32[2,256]{1,0:T(2,128)} %refs_2_.1, f32[32,16,256]{2,1,0:T(8,128)} %refs_3_.1), custom_call_target="tpu_custom_call" | custom-call | tf_op jit(solution)/shard_map/pallas_call | solution.py:367
  84.7 1.1 %shard_map.60 = (f32[1,32,16,256]{3,2,1,0:T(8,128)}, f32[1,32,16,256]{3,2,1,0:T(8,128)}) custom-call(f32[32,32,128]{2,1,0:T(8,128)S(1)} %get-tuple-element.4.middle, f32[32,32,128]{2,1,0:T(8,128)S(1)} %get-tuple-element.5.final), custom_call_target="tpu_custom_call" | custom-call | tf_op jit(solution)/shard_map/pallas_call | solution.py:387

commit v4 on v3

--- a/solution.py
+++ b/solution.py
@@ -146,7 +146,7 @@
 
             @pl.when(ok)
             def _(kind=kind):
-                source = border.at[l // 3] if far_ones and l % 3 == 2 else None
+                source = border.at[l // 3, pl.ds(0, BX)] if far_ones and l % 3 == 2 else None
                 getattr(edge(l, kind, step, source), action)()
 
     def shift(l, kind):
@@ -353,7 +353,7 @@
                 target[0, x, :, pl.ds(128 * half, 128)] = source[x, pl.ds(half, BY, stride=2), :]
         return carry
 
-    lax.fori_loop(0, middle.shape[0], body, 0, unroll=4)
+    lax.fori_loop(0, BX, body, 0, unroll=4)
 
 
 def solution(mesh):
@@ -361,7 +361,7 @@
 
     def shards(start_states, wind_code, wind_profile, vertical_mix):
         block = jax.ShapeDtypeStruct(start_states.shape, jnp.float32)
-        packed = jax.ShapeDtypeStruct((BX, ROWS, 128), jnp.float32)
+        packed = jax.ShapeDtypeStruct((BX + 1, ROWS, 128), jnp.float32)
         field = pltpu.VMEM(packed.shape, jnp.float32)
         any_space, vmem = pl.BlockSpec(memory_space=pl.ANY), pl.BlockSpec(memory_space=pltpu.VMEM)
         middle, final = pl.pallas_call(
@@ -373,8 +373,8 @@
                 pltpu.VMEM((FIELDS, BX + 4, ROWS + 32, 128), jnp.float32),
                 pltpu.VMEM((BX + 4, ROWS + 32, 128), jnp.float32),
                 field, field, field, field, field,
-                pltpu.VMEM((3, BX, 4, 128), jnp.float32),
-                pltpu.VMEM((BX, 4, 128), jnp.float32),
+                pltpu.VMEM((3, BX + 1, 4, 128), jnp.float32),
+                pltpu.VMEM((BX + 1, 4, 128), jnp.float32),
                 pltpu.VMEM((2, 2, BX, BY, 128), jnp.float32),
                 pltpu.VMEM((2, 256), jnp.float32),
                 pltpu.SemaphoreType.DMA,

time: 85.9 us -> 91.3 us (1.063)
  local copies, waits for them, and re-layouts: 0 us -> 4.16 us
  Pallas kernels: 84.5 us -> 85.5 us
    unnamed x0 -> x8, local copies, waits for them, and re-layouts: none -> 4.16 us
    pallas_call x1, Pallas kernels: 83.4 us -> 84.5 us  [shards(): pl.pallas_call(lambda *refs: kernel(shape, *refs), out_shape=(packed, pac...]
where the time goes in v4:
time: 91.3 us; the launch traced here: 91 us
  Pallas kernels  85.5 us (94%)
  local copies, waits for them, and re-layouts  4.16 us (5%)
  between operations  1.3 us (1%)
    pallas_call x1, Pallas kernels, shards(): pl.pallas_call(lambda *refs: kernel(shape, *refs), out_shape=(packed, pac...  84.5 us
    unnamed x8, local copies, waits for them, and re-layouts  4.16 us

profile of v4, /device:TPU:89, one launch (start us, length us, event | category | flops | bytes accessed | tf_op | source)
XLA Modules:
  0.0 91.0 jit_solution(14241113251437581836)
XLA Ops:
  1.3 0.0 copy-start.2
  1.3 1.0 %copy-done.2 = f32[1,32,16,256]{3,2,1,0:T(8,128)S(1)} copy-done((f32[1,32,16,256]{3,2,1,0:T(8,128)S(1)}, f32[1,32,16,256]{3,2,1,0:T(8,128)}, u32[]{:S(2)}) %copy-start.2) | copy-done | bytes 524312
  2.3 0.0 copy-start.3
  2.3 1.0 %copy-done.3 = f32[32,16,256]{2,1,0:T(8,128)S(1)} copy-done((f32[32,16,256]{2,1,0:T(8,128)S(1)}, f32[32,16,256]{2,1,0:T(8,128)}, u32[]{:S(2)}) %copy-start.3) | copy-done | bytes 524312
  3.4 84.5 %shard_map.59 = (f32[33,32,128]{2,1,0:T(8,128)}, f32[33,32,128]{2,1,0:T(8,128)}) custom-call(f32[1,32,16,256]{3,2,1,0:T(8,128)S(1)} %copy-done.2, s32[1,1]{1,0:T(1,128)S(6)} %copy.6.refs_1_, f32[2,256]{1,0:T(2,128)} %refs_2_.1, f32[32,16,256]{2,1,0:T(8,128)S(1)} %copy-done.3), custom_call_target="tpu_custom_call" | custom-call | tf_op jit(solution)/shard_map/pallas_call | solution.py:367
  87.8 0.0 copy-start
  87.9 1.0 %copy-done = f32[33,32,128]{2,1,0:T(8,128)S(1)} copy-done((f32[33,32,128]{2,1,0:T(8,128)S(1)}, f32[33,32,128]{2,1,0:T(8,128)}, u32[]{:S(2)}) %copy-start) | copy-done | bytes 540696
  88.9 0.0 copy-start.1
  88.9 1.0 %copy-done.1 = f32[33,32,128]{2,1,0:T(8,128)S(1)} copy-done((f32[33,32,128]{2,1,0:T(8,128)S(1)}, f32[33,32,128]{2,1,0:T(8,128)}, u32[]{:S(2)}) %copy-start.1) | copy-done | bytes 540696
  89.9 1.1 %shard_map.60 = (f32[1,32,16,256]{3,2,1,0:T(8,128)}, f32[1,32,16,256]{3,2,1,0:T(8,128)}) custom-call(f32[33,32,128]{2,1,0:T(8,128)S(1)} %copy-done, f32[33,32,128]{2,1,0:T(8,128)S(1)} %copy-done.1), custom_call_target="tpu_custom_call" | custom-call | tf_op jit(solution)/shard_map/pallas_call | solution.py:387
Async XLA Ops:
  1.3 1.0 %copy-start.2 = (f32[1,32,16,256]{3,2,1,0:T(8,128)S(1)}, f32[1,32,16,256]{3,2,1,0:T(8,128)}, u32[]{:S(2)}) copy-start(f32[1,32,16,256]{3,2,1,0:T(8,128)} %refs_0_.1) | copy-start | bytes 1572868
  2.3 1.0 %copy-start.3 = (f32[32,16,256]{2,1,0:T(8,128)S(1)}, f32[32,16,256]{2,1,0:T(8,128)}, u32[]{:S(2)}) copy-start(f32[32,16,256]{2,1,0:T(8,128)} %refs_3_.1) | copy-start | bytes 1572868
  87.8 1.0 %copy-start = (f32[33,32,128]{2,1,0:T(8,128)S(1)}, f32[33,32,128]{2,1,0:T(8,128)}, u32[]{:S(2)}) copy-start(f32[33,32,128]{2,1,0:T(8,128)} %get-tuple-element.4.middle) | copy-start | bytes 1622020
  88.9 1.0 %copy-start.1 = (f32[33,32,128]{2,1,0:T(8,128)S(1)}, f32[33,32,128]{2,1,0:T(8,128)}, u32[]{:S(2)}) copy-start(f32[33,32,128]{2,1,0:T(8,128)} %get-tuple-element.5.final) | copy-start | bytes 1622020
